TPU v7x, 512 devices: a whole 4x4x16 slice. The times are simulated.
512 devices in a mesh: side: 2 (over y_hi), group: 64 (over z, y_lo, core), cuts: 4 (over x).
Axes of the slice: x: 4, y: 4 (y_hi: 2, y_lo: 2; y = y_hi * 2 + y_lo), z: 16, core: 2. Of those that a mesh axis runs over, the one named last changes fastest.
Arguments:
- queries: bfloat16 [1024, 4096], P('group', ('side', 'cuts')), may hold values from -8 to 8
- cache_keys: bfloat16 [1024, 8, 64, 512], P('group', ('side', 'cuts')), may hold values from -8 to 8
- cache_values: bfloat16 [1024, 8, 64, 512], P('group', ('side', 'cuts')), may hold values from -6 to 6
- new_keys: bfloat16 [1024, 512], P('group', ('side', 'cuts')), may hold values from -8 to 8
- new_values: bfloat16 [1024, 512], P('group', ('side', 'cuts')), may hold values from -6 to 6
- lengths: int32 [1024], P('group'), may hold values from 1 to 512, as said below
- head_sinks: float32 [64], P(('side', 'cuts')), may hold values from 0 to 6
- attn_proj: bfloat16 [4096, 2880], P(('side', 'cuts'), 'group'), may hold values from -0.625 to 0.625
- residual_in: bfloat16 [1024, 2880], P('group'), may hold values from -8 to 8
- norm_gain: float32 [2880], replicated, may hold values from 0.25 to 1.75
- router: bfloat16 [2880, 32], replicated, may hold values from -0.109375 to 0.109375
- expert_routes: int32 [1024, 4], P('group'), may hold values from 0 to 31, all different within a row; in each aligned block of 16 rows (0 to 15, 16 to 31, ...) at most 4 rows name the same one
- expert_gate: bfloat16 [2880, 92160], P(None, ('side', 'group', 'cuts')), may hold values from -0.109375 to 0.109375
- expert_up: bfloat16 [2880, 92160], P(None, ('side', 'group', 'cuts')), may hold values from -0.109375 to 0.109375
- expert_down: bfloat16 [92160, 2880], P(('side', 'group', 'cuts')), may hold values from -0.109375 to 0.109375
- adapter_in: bfloat16 [2880, 32], replicated, may hold values from -0.109375 to 0.109375
- adapter_gate: bfloat16 [32, 92160], P(None, ('side', 'group', 'cuts')), may hold values from -1 to 1
- adapter_up: bfloat16 [32, 92160], P(None, ('side', 'group', 'cuts')), may hold values from -1 to 1
Outputs:
- hidden_out: bfloat16 [1024, 2880], P('group', 'cuts')
Inputs may be any that keep to these rules, and one draw needn't show every extreme that they name: `expert_routes`: the 16 requests of one index of group name any one expert at most 4 times, a bound that some block reaches. `lengths`: some request has all 512 positions valid.
All inputs are finite; a program needn't handle non-finite values.
Results may differ from a plain program's by a relative error of at most 0.02.
Values may be sent and summed in bfloat16 or wider, within the bound.
No kernel may reach another device: no remote copies, remote signals or barrier semaphores. Data moves between devices by JAX's collectives and lax.ppermute only.
A program may use at most 64 MiB of HBM per device.

v0:
```python
import math

import jax
import jax.numpy as jnp
from jax import lax
from jax.sharding import PartitionSpec as P

FF = 2880
CAP = 4


epsilon = 1e-05


def attention_rows(queries, cache_keys, cache_values, new_keys, new_values, lengths, head_sinks):
    req_count = queries.shape[0]
    kv_count = cache_keys.shape[1]
    head_dim = cache_keys.shape[2]
    cache_len = cache_keys.shape[3]
    head_count = head_sinks.shape[0]
    group_size = head_count // kv_count
    query_rows = queries.reshape(req_count, kv_count, group_size, head_dim)
    fresh_key = new_keys.reshape(req_count, kv_count, head_dim)
    fresh_value = new_values.reshape(req_count, kv_count, head_dim)
    scaling = 1.0 / math.sqrt(head_dim)
    scores = (
        jnp.einsum("rkgd,rkdl->rkgl", query_rows, cache_keys, preferred_element_type=jnp.float32)
        * scaling
    )
    own_score = (
        jnp.einsum("rkgd,rkd->rkg", query_rows, fresh_key, preferred_element_type=jnp.float32)
        * scaling
    )
    validity = (
        lax.broadcasted_iota(jnp.int32, (req_count, 1, 1, cache_len), 3)
        < lengths[:, None, None, None]
    )
    scores = jnp.where(validity, scores, -1e30)
    sink_logit = head_sinks.reshape(1, kv_count, group_size)
    highest = jnp.maximum(jnp.maximum(jnp.max(scores, axis=3), own_score), sink_logit)
    exp_terms = jnp.where(validity, jnp.exp(scores - highest[..., None]), 0.0)
    own_term = jnp.exp(own_score - highest)
    denominator = jnp.sum(exp_terms, axis=3) + own_term + jnp.exp(sink_logit - highest)
    attn_probs = (exp_terms / denominator[..., None]).astype(jnp.bfloat16)
    own_prob = (own_term / denominator).astype(jnp.bfloat16)
    attn_mix = jnp.einsum(
        "rkgl,rkdl->rkgd", attn_probs, cache_values, preferred_element_type=jnp.float32
    )
    attn_mix = (
        attn_mix
        + own_prob.astype(jnp.float32)[..., None] * fresh_value.astype(jnp.float32)[:, :, None, :]
    )
    return attn_mix.astype(jnp.bfloat16).reshape(req_count, head_count * head_dim)


def routing_matrix(expert_table, expert_routes, slot_pos, weights):
    slot_total = CAP
    matched = (expert_routes[None, None, :, :] == expert_table[:, :, None, None]).astype(
        jnp.float32
    )
    slot_hot = (
        slot_pos[:, :, None] == lax.broadcasted_iota(jnp.int32, (1, 1, slot_total), 2)
    ).astype(jnp.float32)
    return jnp.einsum(
        "gjrk,rkc->gjcr",
        matched * weights[None, None, :, :],
        slot_hot,
        precision=lax.Precision.HIGHEST,
    )


def shards(
    queries,
    cache_keys,
    cache_values,
    new_keys,
    new_values,
    lengths,
    head_sinks,
    attn_proj,
    residual_in,
    norm_gain,
    router,
    expert_routes,
    expert_gate,
    expert_up,
    expert_down,
    adapter_in,
    adapter_gate,
    adapter_up,
):
    n_group = lax.axis_size("group")
    n_cuts = lax.axis_size("cuts")
    side_index = lax.axis_index("side")
    cut_index = lax.axis_index("cuts")
    attn_out = attention_rows(
        queries, cache_keys, cache_values, new_keys, new_values, lengths, head_sinks
    )
    req_count = attn_out.shape[0]
    width = residual_in.shape[1]
    quarter = width // n_cuts
    partial_cols = jnp.dot(
        lax.all_gather(attn_out, "group", axis=0, tiled=True),
        attn_proj,
        preferred_element_type=jnp.float32,
    )
    partial_rows = lax.all_to_all(
        partial_cols.astype(jnp.bfloat16), "group", split_axis=0, concat_axis=1, tiled=True
    ).astype(partial_cols.dtype)
    projected = lax.psum(partial_rows.astype(jnp.bfloat16), ("side", "cuts")).astype(jnp.float32)
    middle = residual_in.astype(jnp.float32) + projected
    inverse = lax.rsqrt(jnp.mean(middle * middle, axis=1, keepdims=True) + epsilon)
    normed = (middle * inverse * norm_gain).astype(jnp.bfloat16)
    logits = jnp.dot(normed, router, preferred_element_type=jnp.float32)
    expert_count = router.shape[1]
    chosen = (
        expert_routes[:, :, None] == lax.broadcasted_iota(jnp.int32, (1, 1, expert_count), 2)
    ).astype(jnp.float32)
    picked = jnp.sum(chosen * logits[:, None, :], axis=2)
    raw_gate = jax.nn.sigmoid(picked)
    gate_weights = raw_gate / jnp.sum(raw_gate, axis=1, keepdims=True)
    member = jnp.sum(chosen, axis=1)
    earlier = (
        lax.broadcasted_iota(jnp.int32, (req_count, req_count), 1)
        < lax.broadcasted_iota(jnp.int32, (req_count, req_count), 0)
    ).astype(jnp.float32)
    before = jnp.sum(earlier[:, :, None] * member[None, :, :], axis=1)
    slot_pos = jnp.sum(chosen * before[:, None, :], axis=2).astype(jnp.int32)
    slice_width = expert_gate.shape[1]
    local_count = max(slice_width // FF, 1)
    hidden_local = min(slice_width, FF)
    rank_width = adapter_in.shape[1]
    dest_groups = lax.broadcasted_iota(jnp.int32, (n_group, 1), 0)
    row_base = (side_index * n_group + dest_groups) * n_cuts
    local_table = (row_base + cut_index) * slice_width // FF + lax.broadcasted_iota(
        jnp.int32, (1, local_count), 1
    )
    ones_weight = jnp.ones(gate_weights.shape, jnp.float32)
    gate_cols = expert_gate.reshape(width, local_count, hidden_local)
    up_cols = expert_up.reshape(width, local_count, hidden_local)
    down_rows = expert_down.reshape(local_count, hidden_local, width)
    adapt_gate = adapter_gate.reshape(rank_width, local_count, hidden_local)
    adapt_up = adapter_up.reshape(rank_width, local_count, hidden_local)
    placement = routing_matrix(local_table, expert_routes, slot_pos, ones_weight).astype(
        jnp.bfloat16
    )
    outgoing = jnp.einsum(
        "gjcr,rd->gjcd", placement, normed, preferred_element_type=jnp.float32
    ).astype(jnp.bfloat16)
    row_block = lax.all_to_all(outgoing, "group", split_axis=0, concat_axis=0, tiled=True)
    pre_gate = jnp.einsum(
        "gjcd,djh->gjch", row_block, gate_cols, preferred_element_type=jnp.float32
    )
    pre_up = jnp.einsum("gjcd,djh->gjch", row_block, up_cols, preferred_element_type=jnp.float32)
    low_code = jnp.einsum(
        "gjcd,dr->gjcr", row_block, adapter_in, preferred_element_type=jnp.float32
    ).astype(jnp.bfloat16)
    finish_pre_gate = pre_gate
    finish_pre_up = pre_up
    finish_pre_gate = finish_pre_gate + jnp.einsum(
        "gjcr,rjh->gjch", low_code, adapt_gate, preferred_element_type=jnp.float32
    )
    finish_pre_up = finish_pre_up + jnp.einsum(
        "gjcr,rjh->gjch", low_code, adapt_up, preferred_element_type=jnp.float32
    )
    activated = (
        (finish_pre_up + 1.0) * finish_pre_gate * jax.nn.sigmoid(1.702 * finish_pre_gate)
    ).astype(jnp.bfloat16)
    partial_value = jnp.einsum(
        "gjch,jhd->gjcd", activated, down_rows, preferred_element_type=jnp.float32
    )
    returned = lax.all_to_all(
        partial_value.astype(jnp.bfloat16), "group", split_axis=0, concat_axis=0, tiled=True
    ).astype(partial_value.dtype)
    weighting = routing_matrix(local_table, expert_routes, slot_pos, gate_weights)
    moe_part = jnp.einsum("gjcr,gjcd->rd", weighting, returned, precision=lax.Precision.HIGHEST)
    moe_cols = lax.psum_scatter(
        moe_part.astype(jnp.bfloat16), "cuts", scatter_dimension=1, tiled=True
    )
    moe_total = lax.psum(moe_cols, "side").astype(jnp.float32)
    middle_cols = lax.dynamic_slice_in_dim(middle, cut_index * quarter, quarter, 1)
    return (middle_cols + moe_total).astype(jnp.bfloat16)


def solution(mesh):
    placed = (
        P("group", ("side", "cuts")),
        P("group", ("side", "cuts"), None, None),
        P("group", ("side", "cuts"), None, None),
        P("group", ("side", "cuts")),
        P("group", ("side", "cuts")),
        P("group"),
        P(("side", "cuts")),
        P(("side", "cuts"), "group"),
        P("group", None),
        P(),
        P(),
        P("group", None),
        P(None, ("side", "group", "cuts")),
        P(None, ("side", "group", "cuts")),
        P(("side", "group", "cuts"), None),
        P(),
        P(None, ("side", "group", "cuts")),
        P(None, ("side", "group", "cuts")),
    )
    return jax.shard_map(
        shards, mesh=mesh, in_specs=placed, out_specs=P("group", "cuts"), check_vma=False
    )
```

profile of v0, /device:TPU:32, one launch (start us, length us, event | category | flops | bytes accessed | tf_op | source)
XLA Modules:
  0.0 480.0 jit_solution(1286696299472600859)
XLA Ops:
  6.6 0.9 iota_compare_fusion.4
  8.3 0.8 fusion.76
  9.1 1.6 fusion.85
  12.8 125.6 %all-gather.2.cloned.1.call-done = bf16[1024,512]{1,0:T(8,128)(2,1)} async-done(((bf16[16,512]{1,0:T(8,128)(2,1)}), bf16[1024,512]{1,0:T(8,128)(2,1)}) %all-gather.2.cloned.1.call-update) | async-done | bytes 1048592 | tf_op jit(solution)/shard_map/all_gather | solution.py:103
  138.4 1.6 convolution_convert_fusion.2
  140.3 1.0 reshape.264
  141.3 9.0 %all-to-all-start = ((bf16[64,2,360]{2,1,0:T(2,128)(2,1)}), bf16[64,2,360]{2,1,0:T(2,128)(2,1)S(1)}, u32[]{:S(2)}, u32[]{:S(2)}) async-start(bf16[64,2,360]{2,1,0:T(2,128)(2,1)} %reshape.264), calls=%async_computation | async-start | bytes 196608 | tf_op jit(solution)/shard_map/all_to_all | solution.py:107
  150.7 14.5 %all-to-all-done = bf16[64,2,360]{2,1,0:T(2,128)(2,1)S(1)} async-done(((bf16[64,2,360]{2,1,0:T(2,128)(2,1)}), bf16[64,2,360]{2,1,0:T(2,128)(2,1)S(1)}, u32[]{:S(2)}, u32[]{:S(2)}) %all-to-all-start) | async-done | bytes 92192 | tf_op jit(solution)/shard_map/all_to_all | solution.py:107
  165.6 1.0 all_to_all.23
  166.6 88.7 %all-reduce.2.cloned.1.call-done = bf16[16,2880]{1,0:T(8,128)(2,1)} async-done(((bf16[16,2880]{1,0:T(8,128)(2,1)}), bf16[16,2880]{1,0:T(8,128)(2,1)}) %all-reduce.2.cloned.1.call-update) | async-done | bytes 92176 | tf_op jit(solution)/shard_map/psum | solution.py:110
  255.3 1.0 convert_add_fusion
  256.3 1.1 fusion.84
  258.0 1.5 fusion
  259.5 1.2 copy.46
  260.6 87.5 %all_to_all.29 = bf16[64,1,4,2880]{3,2,1,0:T(4,128)(2,1)S(1)} all-to-all(bf16[64,1,4,2880]{3,2,1,0:T(4,128)(2,1)S(1)} %copy.46), channel_id=1, replica_groups=mesh['side'=2,'group'=64,'cuts'=4] {'group'}, dimensions={0} | all-to-all | bytes 2949120 | tf_op jit(solution)/shard_map/all_to_all | solution.py:150
  348.2 0.8 fusion.34
  350.1 4.2 fusion.1
  354.3 3.7 copy.48
  358.0 6.4 %all-to-all-start.2 = ((bf16[64,1,4,2880]{3,2,1,0:T(4,128)(2,1)}), bf16[64,1,4,2880]{3,2,1,0:T(4,128)(2,1)S(1)}, u32[]{:S(2)}, u32[]{:S(2)}) async-start(bf16[64,1,4,2880]{3,2,1,0:T(4,128)(2,1)} %copy.48), calls=%async_computation.2 | async-start | bytes 3014656 | tf_op jit(solution)/shard_map/all_to_all | solution.py:172
  364.8 74.2 %all-to-all-done.2 = bf16[64,1,4,2880]{3,2,1,0:T(4,128)(2,1)S(1)} async-done(((bf16[64,1,4,2880]{3,2,1,0:T(4,128)(2,1)}), bf16[64,1,4,2880]{3,2,1,0:T(4,128)(2,1)S(1)}, u32[]{:S(2)}, u32[]{:S(2)}) %all-to-all-start.2) | async-done | bytes 1474592 | tf_op jit(solution)/shard_map/all_to_all | solution.py:172
  439.8 1.2 copy.53
  441.0 19.4 %reduce-scatter.4.cloned.1.call-done = bf16[720,16]{1,0:T(8,128)(2,1)} async-done(((bf16[2880,16]{1,0:T(8,128)(2,1)}), bf16[720,16]{1,0:T(8,128)(2,1)}) %reduce-scatter.4.cloned.1.call-update) | async-done | bytes 23056
  460.4 1.0 copy.54
  461.4 11.4 %psum.15 = bf16[16,720]{1,0:T(8,128)(2,1)S(1)} all-reduce(bf16[16,720]{1,0:T(8,128)(2,1)S(1)} %copy.54), channel_id=1, replica_groups=mesh['side'=2,'group'=64,'cuts'=4] {'side'}, use_global_device_ids=true, to_apply=%region_10.11 | all-reduce | flops 11520 | bytes 46080 | tf_op jit(solution)/shard_map/psum | solution.py:180
  (61 shorter events, 7.2 us)
Async XLA Ops:
  6.5 343.6 %copy-start = (bf16[180,2880]{1,0:T(8,128)(2,1)S(1)}, bf16[180,2880]{1,0:T(8,128)(2,1)}, u32[]{:S(2)}) copy-start(bf16[180,2880]{1,0:T(8,128)(2,1)} %param.32) | copy-start | bytes 3110404
  6.5 5.0 %copy-start.9 = (f32[8]{0:T(128)S(1)}, f32[8]{0:T(128)}, u32[]{:S(2)}) copy-start(f32[8]{0:T(128)} %param.24) | copy-start | bytes 100
  6.5 5.0 %copy-start.8 = (bf16[16,64]{1,0:T(8,128)(2,1)S(1)}, bf16[16,64]{1,0:T(8,128)(2,1)}, u32[]{:S(2)}) copy-start(bf16[16,64]{1,0:T(8,128)(2,1)} %param.22) | copy-start | bytes 6148
  6.5 5.0 %copy-start.11 = (bf16[16,1,64,512]{3,2,1,0:T(8,128)(2,1)S(1)}, bf16[16,1,64,512]{3,2,1,0:T(8,128)(2,1)}, u32[]{:S(2)}) copy-start(bf16[16,1,64,512]{3,2,1,0:T(8,128)(2,1)} %param.20) | copy-start | bytes 3145732
  6.5 131.9 %all-gather.2.cloned.1.call-start = ((), (), s32[]{:S(2)}) async-start(), calls=%async_computation.4 | async-start | bytes 1064960 | tf_op jit(solution)/shard_map/all_gather | solution.py:103
  9.1 129.3 %copy-start.4 = (bf16[512,45]{0,1:T(8,128)(2,1)S(1)}, bf16[512,45]{0,1:T(8,128)(2,1)}, u32[]{:S(2)}) copy-start(bf16[512,45]{0,1:T(8,128)(2,1)} %param.25) | copy-start | bytes 138244
  12.0 138.3 %copy-start.5 = (s32[16,4]{0,1:T(4,128)S(1)}, s32[16,4]{0,1:T(4,128)}, u32[]{:S(2)}) copy-start(s32[16,4]{0,1:T(4,128)} %param.29) | copy-start | bytes 772
  12.8 242.5 %copy-start.1 = (bf16[16,2880]{1,0:T(8,128)(2,1)S(1)}, bf16[16,2880]{1,0:T(8,128)(2,1)}, u32[]{:S(2)}) copy-start(bf16[16,2880]{1,0:T(8,128)(2,1)} %param.26) | copy-start | bytes 276484
  140.1 116.3 %copy-start.2 = (bf16[2880,32]{0,1:T(8,128)(2,1)S(1)}, bf16[2880,32]{0,1:T(8,128)(2,1)}, u32[]{:S(2)}) copy-start(bf16[2880,32]{0,1:T(8,128)(2,1)} %param.28) | copy-start | bytes 552964
  140.1 116.3 %copy-start.3 = (f32[2880]{0:T(1024)S(1)}, f32[2880]{0:T(1024)}, u32[]{:S(2)}) copy-start(f32[2880]{0:T(1024)} %param.27) | copy-start | bytes 34564
  141.3 23.9 %all-to-all-start = ((bf16[64,2,360]{2,1,0:T(2,128)(2,1)}), bf16[64,2,360]{2,1,0:T(2,128)(2,1)S(1)}, u32[]{:S(2)}, u32[]{:S(2)}) async-start(bf16[64,2,360]{2,1,0:T(2,128)(2,1)} %reshape.264), calls=%async_computation | async-start | bytes 196608 | tf_op jit(solution)/shard_map/all_to_all | solution.py:107
  150.3 104.9 %all-reduce.2.cloned.1.call-start = ((), (), s32[]{:S(2)}) async-start(), calls=%async_computation.5 | async-start | bytes 188416 | tf_op jit(solution)/shard_map/psum | solution.py:110
  260.6 87.5 %copy-start.12 = (bf16[2880,32]{0,1:T(8,128)(2,1)S(1)}, bf16[2880,32]{0,1:T(8,128)(2,1)}, u32[]{:S(2)}) copy-start(bf16[2880,32]{0,1:T(8,128)(2,1)} %param.33) | copy-start | bytes 552964
  348.2 0.9 copy-start.6
  348.2 1.1 copy-start.7
  348.2 1.3 copy-start.10
  358.0 81.0 %all-to-all-start.2 = ((bf16[64,1,4,2880]{3,2,1,0:T(4,128)(2,1)}), bf16[64,1,4,2880]{3,2,1,0:T(4,128)(2,1)S(1)}, u32[]{:S(2)}, u32[]{:S(2)}) async-start(bf16[64,1,4,2880]{3,2,1,0:T(4,128)(2,1)} %copy.48), calls=%async_computation.2 | async-start | bytes 3014656 | tf_op jit(solution)/shard_map/all_to_all | solution.py:172
  364.4 96.0 %reduce-scatter.4.cloned.1.call-start = ((), (), s32[]{:S(2)}) async-start(), calls=%async_computation.6 | async-start | bytes 921600
Sparse Core Ops, SparseCore 0:
  12.9 125.4 all-gather.1
  166.7 88.5 all-reduce.1
  441.1 19.2 reduce-scatter.3
where the time goes:
time: 481 us; the launch traced here: 480 us
  waiting for transfers between devices  322 us (67%)
  blocking collectives  99 us (21%)
  starting transfers between devices  15.5 us (3%)
  matrix products  14.4 us (3%)
  between operations  13.4 us (3%)
  local copies, waits for them, and re-layouts  11.4 us (2%)
    all_gather x1, waiting for transfers between devices, shards(): lax.all_gather(attn_out, 'group', axis=0, tiled=True)  126 us
    psum x1, waiting for transfers between devices, shards(): lax.psum(partial_rows.astype(jnp.bfloat16), ('side', 'cuts'))  88.7 us
    all_to_all x1, blocking collectives, shards(): lax.all_to_all(outgoing, 'group', split_axis=0, concat_axis=0, tiled=True)  87.5 us
    all_to_all x1, waiting for transfers between devices, shards(): lax.all_to_all(partial_value.astype(jnp.bfloat16), 'group', split_axis=0,...  74.2 us
    unnamed x4, waiting for transfers between devices  19.4 us
    all_to_all x1, waiting for transfers between devices, shards(): lax.all_to_all(partial_cols.astype(jnp.bfloat16), 'group', split_axis=0,...  14.5 us
    psum x1, blocking collectives, shards(): moe_total = lax.psum(moe_cols, 'side').astype(jnp.float32)  11.4 us
  transfers between devices with their start and end apart: 5, of which 5 were waited for; matrix products, arithmetic and copies ran while one was open for 0% of the time, Pallas kernels for 0%

commit v1 on v0

v1 whole, which is shorter than its diff:
```python
import math

import jax
import jax.numpy as jnp
from jax import lax
from jax.sharding import Mesh, PartitionSpec as P

CAP = 4
EPSILON = 1e-05
F32 = jnp.float32
BF16 = jnp.bfloat16


def attention_rows(queries, cache_keys, cache_values, new_keys, new_values, lengths, head_sinks):
    req_count = queries.shape[0]
    kv_count = cache_keys.shape[1]
    head_dim = cache_keys.shape[2]
    cache_len = cache_keys.shape[3]
    head_count = head_sinks.shape[0]
    group_size = head_count // kv_count
    query_rows = queries.reshape(req_count, kv_count, group_size, head_dim)
    fresh_key = new_keys.reshape(req_count, kv_count, head_dim)
    fresh_value = new_values.reshape(req_count, kv_count, head_dim)
    scaling = 1.0 / math.sqrt(head_dim)
    scores = (
        jnp.einsum("rkgd,rkdl->rkgl", query_rows, cache_keys, preferred_element_type=F32) * scaling
    )
    own_score = (
        jnp.einsum("rkgd,rkd->rkg", query_rows, fresh_key, preferred_element_type=F32) * scaling
    )
    validity = (
        lax.broadcasted_iota(jnp.int32, (req_count, 1, 1, cache_len), 3)
        < lengths[:, None, None, None]
    )
    scores = jnp.where(validity, scores, -1e30)
    sink_logit = head_sinks.reshape(1, kv_count, group_size)
    highest = jnp.maximum(jnp.maximum(jnp.max(scores, axis=3), own_score), sink_logit)
    exp_terms = jnp.where(validity, jnp.exp(scores - highest[..., None]), 0.0)
    own_term = jnp.exp(own_score - highest)
    denominator = jnp.sum(exp_terms, axis=3) + own_term + jnp.exp(sink_logit - highest)
    attn_probs = (exp_terms / denominator[..., None]).astype(BF16)
    own_prob = (own_term / denominator).astype(BF16)
    attn_mix = jnp.einsum("rkgl,rkdl->rkgd", attn_probs, cache_values, preferred_element_type=F32)
    attn_mix = attn_mix + own_prob.astype(F32)[..., None] * fresh_value.astype(F32)[:, :, None, :]
    return attn_mix.astype(BF16).reshape(req_count, head_count * head_dim)


def exchange(array, axes):
    return lax.all_to_all(array, axes, split_axis=0, concat_axis=0, tiled=True)


def slot_hot(routes, experts):
    rows = routes.shape[1]
    member = jnp.any(routes[None] == experts[:, None, None, None], axis=3)
    earlier = (
        lax.broadcasted_iota(jnp.int32, (rows, rows), 0)
        < lax.broadcasted_iota(jnp.int32, (rows, rows), 1)
    ).astype(BF16)
    before = jnp.einsum(
        "ebr,rq->ebq", member.astype(BF16), earlier, preferred_element_type=F32
    ).astype(jnp.int32)
    slots = lax.broadcasted_iota(jnp.int32, (1, 1, CAP, 1), 2)
    return (member[:, :, None, :] & (before[:, :, None, :] == slots)).astype(BF16)


def shards(
    queries,
    cache_keys,
    cache_values,
    new_keys,
    new_values,
    lengths,
    head_sinks,
    attn_proj,
    residual_in,
    norm_gain,
    router,
    expert_routes,
    expert_gate,
    expert_up,
    expert_down,
    adapter_in,
    adapter_gate,
    adapter_up,
):
    planes = lax.axis_size("z")
    n_cuts = lax.axis_size("cuts")
    n_side = lax.axis_size("side")
    n_ylo = lax.axis_size("ylo")
    side = lax.axis_index("side")
    plane = lax.axis_index("z")
    ylo = lax.axis_index("ylo")
    cut = lax.axis_index("cuts")
    rows, width = residual_in.shape
    topk = expert_routes.shape[1]
    heads_in, piece = attn_proj.shape
    strip = width // planes
    quarter = width // n_cuts
    swap = [(0, 1), (1, 0)]

    plane_proj = exchange(
        jnp.broadcast_to(attn_proj.T[None], (4, piece, heads_in)), ("ylo", "core")
    ).reshape(strip, heads_in)
    gate_t = jnp.concatenate([expert_gate.T, lax.ppermute(expert_gate.T, "core", swap)], 0)
    up_t = jnp.concatenate([expert_up.T, lax.ppermute(expert_up.T, "core", swap)], 0)
    down = jnp.concatenate([expert_down, lax.ppermute(expert_down, "core", swap)], 0)
    adapt_gate = jnp.concatenate([adapter_gate, lax.ppermute(adapter_gate, "core", swap)], 1)
    adapt_up = jnp.concatenate([adapter_up, lax.ppermute(adapter_up, "core", swap)], 1)

    attn_out = attention_rows(
        queries, cache_keys, cache_values, new_keys, new_values, lengths, head_sinks
    )

    residual = residual_in.reshape(rows, planes, n_cuts, piece)
    residual = lax.dynamic_index_in_dim(residual, cut, 2, keepdims=False).transpose(1, 0, 2)
    payload = jnp.concatenate(
        [
            jnp.broadcast_to(attn_out[None], (planes, rows, heads_in)),
            residual,
            jnp.broadcast_to(expert_routes.astype(BF16)[None], (planes, rows, topk)),
            jnp.zeros((planes, rows, 128 - piece - topk), BF16),
        ],
        axis=2,
    )
    held = exchange(payload, "z").reshape(planes * rows, heads_in + 128)
    line = lax.broadcasted_iota(jnp.int32, (strip, 128), 1)
    column = lax.broadcasted_iota(jnp.int32, (strip, 128), 0)
    residual_part = jnp.where((column == cut * piece + line) & (line < piece), 1.0 / n_side, 0.0)
    weights = jnp.concatenate([plane_proj, residual_part.astype(BF16)], 1)
    partial = lax.dot_general(held, weights, (((1,), (1,)), ((), ())), preferred_element_type=F32)
    partial = partial.astype(BF16).reshape(1, n_cuts, rows * planes // n_cuts, strip)
    partial = jnp.broadcast_to(partial, (n_side,) + partial.shape[1:])
    partial = exchange(partial.reshape((n_side * n_cuts,) + partial.shape[2:]), ("side", "cuts"))
    middle = jnp.sum(partial.astype(F32), axis=0).astype(BF16)

    blocks = planes // n_cuts
    experts = side * planes + jnp.arange(planes)
    routes = held[:, heads_in + piece : heads_in + piece + topk].reshape(n_cuts, blocks, rows, topk)
    routes = lax.dynamic_index_in_dim(routes, cut, 0, keepdims=False)
    hot = slot_hot(routes.astype(jnp.int32), experts)
    source = jnp.concatenate([middle.reshape(blocks, rows, strip), routes], 2)
    outgoing = jnp.einsum("zktr,krd->zktd", hot, source, preferred_element_type=F32).astype(BF16)
    outgoing = outgoing.reshape(planes, blocks * CAP, strip + topk)
    arrived = exchange(outgoing, "z")
    row_part = arrived[:, :, :strip].transpose(1, 0, 2).reshape(blocks * CAP, width)
    row_part = jnp.concatenate([row_part, arrived[0, :, strip:]], 1)
    peers = n_ylo * n_cuts
    row_block = exchange(jnp.broadcast_to(row_part[None], (peers,) + row_part.shape), ("ylo", "cuts"))
    row_block = row_block.reshape(-1, width + topk)

    middle_rows = row_block[:, :width].astype(F32)
    row_routes = row_block[:, width:].astype(jnp.int32)
    inverse = lax.rsqrt(jnp.mean(middle_rows * middle_rows, axis=1, keepdims=True) + EPSILON)
    normed = (middle_rows * inverse * norm_gain).astype(BF16)
    raw = jax.nn.sigmoid(jnp.dot(normed, router, preferred_element_type=F32))
    expert = side * planes + plane
    names = lax.broadcasted_iota(jnp.int32, (1, router.shape[1]), 1)
    named = jnp.any(row_routes[:, :, None] == names[:, None, :], axis=1)
    row_weight = jnp.sum(jnp.where(names == expert, raw, 0.0), axis=1) / jnp.sum(
        jnp.where(named, raw, 0.0), axis=1
    )
    first = (row_routes[:, 0] == expert).astype(F32)
    low_code = jnp.dot(normed, adapter_in, preferred_element_type=F32).astype(BF16)
    nt = (((1,), (1,)), ((), ()))
    pre_gate = lax.dot_general(normed, gate_t, nt, preferred_element_type=F32)
    pre_gate = pre_gate + jnp.dot(low_code, adapt_gate, preferred_element_type=F32)
    pre_up = lax.dot_general(normed, up_t, nt, preferred_element_type=F32)
    pre_up = pre_up + jnp.dot(low_code, adapt_up, preferred_element_type=F32)
    activated = ((pre_up + 1.0) * pre_gate * jax.nn.sigmoid(1.702 * pre_gate)).astype(BF16)
    value = jnp.dot(activated, down, preferred_element_type=F32).astype(BF16)

    own_rows = value.shape[0] // n_ylo
    value = value.reshape(n_ylo, own_rows, n_cuts, quarter).transpose(0, 2, 1, 3)
    value = exchange(value.reshape(peers, own_rows, quarter), ("ylo", "cuts"))
    total = jnp.sum(value.astype(F32), axis=0)
    own_weight = lax.dynamic_slice_in_dim(row_weight, ylo * own_rows, own_rows)
    own_first = lax.dynamic_slice_in_dim(first, ylo * own_rows, own_rows)
    own_middle = lax.dynamic_slice(
        row_block, (ylo * own_rows, cut * quarter), (own_rows, quarter)
    ).astype(F32)
    total = (total * own_weight[:, None] + own_middle * own_first[:, None]).astype(BF16)
    returned = exchange(total.reshape(planes, CAP, quarter), "z")
    own_hot = slot_hot(expert_routes[None], experts)[:, 0]
    out = jnp.einsum("ztr,ztd->rd", own_hot, returned, preferred_element_type=F32).astype(BF16)
    other = lax.ppermute(out, "side", swap)
    return (out.astype(F32) + other.astype(F32)).astype(BF16)


def solution(mesh):
    fine = Mesh(mesh.devices.reshape(2, 16, 2, 2, 4), ("side", "z", "ylo", "core", "cuts"))
    group = ("z", "ylo", "core")
    heads = ("side", "cuts")
    hidden = ("side", "z", "ylo", "core", "cuts")
    placed = (
        P(group, heads),
        P(group, heads, None, None),
        P(group, heads, None, None),
        P(group, heads),
        P(group, heads),
        P(group),
        P(heads),
        P(heads, group),
        P(group, None),
        P(),
        P(),
        P(group, None),
        P(None, hidden),
        P(None, hidden),
        P(hidden, None),
        P(),
        P(None, hidden),
        P(None, hidden),
    )
    return jax.shard_map(
        shards, mesh=fine, in_specs=placed, out_specs=P(group, "cuts"), check_vma=False
    )
```

time: 481 us -> 156 us (0.32)
  waiting for transfers between devices: 322 us -> 59.1 us
  blocking collectives: 99 us -> 19.8 us
  starting transfers between devices: 15.5 us -> 52.8 us
  between operations: 13.4 us -> 0.49 us
    all_gather x1 -> x0, waiting for transfers between devices: 126 us -> none  [shards(): lax.all_gather(attn_out, 'group', axis=0, tiled=True)]
    psum x1 -> x0, waiting for transfers between devices: 88.7 us -> none  [shards(): lax.psum(partial_rows.astype(jnp.bfloat16), ('side', 'cuts'))]
    all_to_all x1, blocking collectives: 87.5 us -> 19.8 us  [exchange(): return lax.all_to_all(array, axes, split_axis=0, concat_axis=0, tiled=True)]
    all_to_all x2 -> x6, waiting for transfers between devices: 88.7 us -> 54.5 us  [exchange(): return lax.all_to_all(array, axes, split_axis=0, concat_axis=0, tiled=True)]
    all_to_all x2 -> x6, starting transfers between devices: 15.4 us -> 39.6 us  [exchange(): return lax.all_to_all(array, axes, split_axis=0, concat_axis=0, tiled=True)]
    unnamed x4 -> x0, waiting for transfers between devices: 19.4 us -> none
    ppermute x0 -> x6, starting transfers between devices: none -> 13.3 us  [the longest x1 2.67 us: shards(): other = lax.ppermute(out, 'side', swap)]
    psum x1 -> x0, blocking collectives: 11.4 us -> none  [shards(): moe_total = lax.psum(moe_cols, 'side').astype(jnp.float32)]
  transfers between devices with their start and end apart: 5 -> 12, of which waited for: 5 -> 5; matrix products, arithmetic and copies ran while one was open for 0% -> 7% of each run, Pallas kernels for 0% -> 0%
where the time goes in v1:
time: 156 us; the launch traced here: 155 us
  waiting for transfers between devices  59.1 us (38%)
  starting transfers between devices  52.8 us (34%)
  blocking collectives  19.8 us (13%)
  local copies, waits for them, and re-layouts  9.79 us (6%)
  matrix products  9.71 us (6%)
  other arithmetic  3.49 us (2%)
    all_to_all x6, waiting for transfers between devices, exchange(): return lax.all_to_all(array, axes, split_axis=0, concat_axis=0, tiled=True)  54.5 us
    all_to_all x6, starting transfers between devices, exchange(): return lax.all_to_all(array, axes, split_axis=0, concat_axis=0, tiled=True)  39.6 us
    all_to_all x1, blocking collectives, exchange(): return lax.all_to_all(array, axes, split_axis=0, concat_axis=0, tiled=True)  19.8 us
    ppermute x1, waiting for transfers between devices, shards(): other = lax.ppermute(out, 'side', swap)  4.55 us
    dot_general x1, matrix products, shards(): value = jnp.dot(activated, down, preferred_element_type=F32).astype(BF16)  3.87 us
  transfers between devices with their start and end apart: 12, of which 5 were waited for; matrix products, arithmetic and copies ran while one was open for 7% of the time, Pallas kernels for 0%

profile of v1, /device:TPU:32, one launch (start us, length us, event | category | flops | bytes accessed | tf_op | source)
XLA Modules:
  0.0 155.1 jit_solution(1757038663491058187)
XLA Ops:
  0.0 1.6 %broadcast_in_dim.99 = bf16[4,45,512]{2,1,0:T(8,128)(2,1)} broadcast(bf16[45,512]{1,0:T(8,128)(2,1)} %bitcast.76), dimensions={1,2} | broadcast | bytes 230400 | tf_op jit(solution)/shard_map/broadcast_in_dim | solution.py:102
  1.6 3.4 %all-to-all-start.1 = ((bf16[4,45,512]{2,1,0:T(8,128)(2,1)}), bf16[4,45,512]{2,1,0:T(8,128)(2,1)S(1)}, u32[]{:S(2)}, u32[]{:S(2)}) async-start(bf16[4,45,512]{2,1,0:T(8,128)(2,1)} %broadcast_in_dim.99), calls=%async_computation.1 | async-start | bytes 393216 | tf_op jit(solution)/shard_map/all_to_all | solution.py:49
  5.8 1.6 %reshape.187 = bf16[16,16,4,45]{3,2,1,0:T(4,128)(2,1)S(1)} reshape(bf16[16,2880]{1,0:T(8,128)(2,1)} %param.26) | data formatting | bytes 184320 | tf_op jit(solution)/shard_map/reshape | solution.py:114
  10.3 15.2 %all-to-all-start = ((bf16[16,16,640]{2,1,0:T(8,128)(2,1)}), bf16[16,16,640]{2,1,0:T(8,128)(2,1)S(1)}, u32[]{:S(2)}, u32[]{:S(2)}) async-start(bf16[16,16,640]{2,1,0:T(8,128)(2,1)} %maximum_maximum_fusion), calls=%async_computation | async-start | bytes 655360 | tf_op jit(solution)/shard_map/all_to_all | solution.py:49
  25.6 20.4 %all-to-all-done = bf16[16,16,640]{2,1,0:T(8,128)(2,1)S(1)} async-done(((bf16[16,16,640]{2,1,0:T(8,128)(2,1)}), bf16[16,16,640]{2,1,0:T(8,128)(2,1)S(1)}, u32[]{:S(2)}, u32[]{:S(2)}) %all-to-all-start) | async-done | bytes 327712 | tf_op jit(solution)/shard_map/all_to_all | solution.py:49
  47.4 6.9 %all-to-all-start.2 = ((bf16[8,64,180]{2,1,0:T(8,128)(2,1)}), bf16[8,64,180]{2,1,0:T(8,128)(2,1)S(1)}, u32[]{:S(2)}, u32[]{:S(2)}) async-start(bf16[8,64,180]{2,1,0:T(8,128)(2,1)} %bitcast.9), calls=%async_computation.2 | async-start | bytes 524288 | tf_op jit(solution)/shard_map/all_to_all | solution.py:49
  54.5 8.6 %all-to-all-done.2 = bf16[8,64,180]{2,1,0:T(8,128)(2,1)S(1)} async-done(((bf16[8,64,180]{2,1,0:T(8,128)(2,1)}), bf16[8,64,180]{2,1,0:T(8,128)(2,1)S(1)}, u32[]{:S(2)}, u32[]{:S(2)}) %all-to-all-start.2) | async-done | bytes 184352 | tf_op jit(solution)/shard_map/all_to_all | solution.py:49
  63.4 19.8 %all_to_all.35 = bf16[16,16,184]{2,1,0:T(8,128)(2,1)S(1)} all-to-all(bf16[16,16,184]{2,1,0:T(8,128)(2,1)S(1)} %copy.63), channel_id=1, replica_groups=mesh['side'=2,'z'=16,'ylo'=2,'core'=2,'cuts'=4] {'z'}, dimensions={0} | all-to-all | bytes 188416 | tf_op jit(solution)/shard_map/all_to_all | solution.py:49
  84.5 3.7 %all-to-all-start.4 = ((bf16[8,16,2884]{2,1,0:T(8,128)(2,1)}), bf16[8,16,2884]{2,1,0:T(8,128)(2,1)S(1)}, u32[]{:S(2)}, u32[]{:S(2)}) async-start(bf16[8,16,2884]{2,1,0:T(8,128)(2,1)} %broadcast_in_dim.104), calls=%async_computation.4 | async-start | bytes 1507328 | tf_op jit(solution)/shard_map/all_to_all | solution.py:49
  88.2 1.9 %collective-permute-start.4 = (bf16[180,2880]{1,0:T(8,128)(2,1)}, bf16[180,2880]{1,0:T(8,128)(2,1)}, u32[]{:S(2)}, u32[]{:S(2)}) collective-permute-start(bf16[180,2880]{1,0:T(8,128)(2,1)} %param.32), channel_id=1, source_target_pairs={{0,4},{4,0},{1,5},{5,1},{2,6},{6,2},{3,7},{7,3},{8,12},{12,8},{9,1... | collective-permute-start | bytes 3110408 | tf_op jit(solution)/shard_map/ppermute | solution.py:106
  90.1 2.4 %collective-permute-start.3 = (bf16[32,180]{1,0:T(8,128)(2,1)S(1)}, bf16[32,180]{1,0:T(8,128)(2,1)S(1)}, u32[]{:S(2)}, u32[]{:S(2)}) collective-permute-start(bf16[32,180]{1,0:T(8,128)(2,1)S(1)} %copy-done.2), channel_id=1, source_target_pairs={{0,4},{4,0},{1,5},{5,1},{2,6},{6,2},{3,7},{7,3},{8,12},{12,8},{9,1... | collective-permute-start | bytes 34568 | tf_op jit(solution)/shard_map/ppermute | solution.py:107
  92.6 1.9 %collective-permute-start.2 = (bf16[180,2880]{1,0:T(8,128)(2,1)}, bf16[180,2880]{1,0:T(8,128)(2,1)}, u32[]{:S(2)}, u32[]{:S(2)}) collective-permute-start(bf16[180,2880]{1,0:T(8,128)(2,1)} %bitcast.22), channel_id=1, source_target_pairs={{0,4},{4,0},{1,5},{5,1},{2,6},{6,2},{3,7},{7,3},{8,12},{12,8},{9,1... | collective-permute-start | bytes 3110408 | tf_op jit(solution)/shard_map/ppermute | solution.py:104
  94.5 2.4 %collective-permute-start.1 = (bf16[32,180]{1,0:T(8,128)(2,1)S(1)}, bf16[32,180]{1,0:T(8,128)(2,1)S(1)}, u32[]{:S(2)}, u32[]{:S(2)}) collective-permute-start(bf16[32,180]{1,0:T(8,128)(2,1)S(1)} %copy-done.3), channel_id=1, source_target_pairs={{0,4},{4,0},{1,5},{5,1},{2,6},{6,2},{3,7},{7,3},{8,12},{12,8},{9,1... | collective-permute-start | bytes 34568 | tf_op jit(solution)/shard_map/ppermute | solution.py:108
  96.9 1.9 %collective-permute-start = (bf16[180,2880]{1,0:T(8,128)(2,1)}, bf16[180,2880]{1,0:T(8,128)(2,1)}, u32[]{:S(2)}, u32[]{:S(2)}) collective-permute-start(bf16[180,2880]{1,0:T(8,128)(2,1)} %bitcast.21), channel_id=1, source_target_pairs={{0,4},{4,0},{1,5},{5,1},{2,6},{6,2},{3,7},{7,3},{8,12},{12,8},{9,1... | collective-permute-start | bytes 3110408 | tf_op jit(solution)/shard_map/ppermute | solution.py:105
  100.2 2.4 %fusion.15 = f32[128,360]{0,1:T(8,128)S(1)} fusion(f32[128,360]{0,1:T(8,128)S(1)} %fusion.72, bf16[180,2880]{1,0:T(8,128)(2,1)} %collective-permute-done.2, bf16[180,2880]{1,0:T(8,128)(2,1)} %bitcast.22, f32[2880]{0:T(1024)S(1)} %copy-done.11, f32[128]{0:T(128)S(1)} %add_rsqrt_fusion, bf16[128,2884]{1,0:T(8,128)(2,1)S(1)} %bitcast.62), kind=kOutput, calls=%fused_computation.21 | convolution fusion | flops 271088640 | bytes 3192576 | tf_op jit(solution)/shard_map/dot_general | solution.py:165
  102.7 3.9 %convolution_convert_fusion = bf16[128,2880]{0,1:T(8,128)(2,1)S(1)} fusion(bf16[180,2880]{1,0:T(8,128)(2,1)} %collective-permute-done.4, bf16[180,2880]{1,0:T(8,128)(2,1)} %param.32, f32[128,360]{0,1:T(8,128)S(1)} %fusion.15, f32[128,360]{0,1:T(8,128)S(1)} %fusion.68, bf16[180,2880]{1,0:T(8,128)(2,1)} %collective-permute-done, bf16[180,2880]{1,0:T(8,128)(2,1)} %bitcast.21, ...), kind=kOutput, calls=%fused_computation | convolution fusion | flops 541393920 | bytes 6003456 | tf_op jit(solution)/shard_map/dot_general | solution.py:170
  106.9 1.1 reshape.196
  108.1 1.0 copy.68
  109.0 5.8 %all-to-all-start.5 = ((bf16[8,64,720]{2,1,0:T(8,128)(2,1)}), bf16[8,64,720]{2,1,0:T(8,128)(2,1)S(1)}, u32[]{:S(2)}, u32[]{:S(2)}) async-start(bf16[8,64,720]{2,1,0:T(8,128)(2,1)} %bitcast.24), calls=%async_computation.5 | async-start | bytes 1572864 | tf_op jit(solution)/shard_map/all_to_all | solution.py:49
  115.7 12.6 %all-to-all-done.5 = bf16[8,64,720]{2,1,0:T(8,128)(2,1)S(1)} async-done(((bf16[8,64,720]{2,1,0:T(8,128)(2,1)}), bf16[8,64,720]{2,1,0:T(8,128)(2,1)S(1)}, u32[]{:S(2)}, u32[]{:S(2)}) %all-to-all-start.5) | async-done | bytes 737312 | tf_op jit(solution)/shard_map/all_to_all | solution.py:49
  129.2 4.6 %all-to-all-start.6 = ((bf16[16,4,720]{2,1,0:T(4,128)(2,1)}), bf16[16,4,720]{2,1,0:T(4,128)(2,1)S(1)}, u32[]{:S(2)}, u32[]{:S(2)}) async-start(bf16[16,4,720]{2,1,0:T(4,128)(2,1)} %reshape.198), calls=%async_computation.6 | async-start | bytes 196608 | tf_op jit(solution)/shard_map/all_to_all | solution.py:49
  134.2 12.8 %all-to-all-done.6 = bf16[16,4,720]{2,1,0:T(4,128)(2,1)S(1)} async-done(((bf16[16,4,720]{2,1,0:T(4,128)(2,1)}), bf16[16,4,720]{2,1,0:T(4,128)(2,1)S(1)}, u32[]{:S(2)}, u32[]{:S(2)}) %all-to-all-start.6) | async-done | bytes 92192 | tf_op jit(solution)/shard_map/all_to_all | solution.py:49
  147.3 2.7 %collective-permute-start.5 = (bf16[16,720]{1,0:T(8,128)(2,1)S(1)}, bf16[16,720]{1,0:T(8,128)(2,1)S(1)}, u32[]{:S(2)}, u32[]{:S(2)}) collective-permute-start(bf16[16,720]{1,0:T(8,128)(2,1)S(1)} %fusion.34), channel_id=1, source_target_pairs={{0,256},{256,0},{1,257},{257,1},{2,258},{258,2},{3,259},{259,3},{4... | collective-permute-start | bytes 69128 | tf_op jit(solution)/shard_map/ppermute | solution.py:185
  150.0 4.5 %collective-permute-done.5 = bf16[16,720]{1,0:T(8,128)(2,1)S(1)} collective-permute-done((bf16[16,720]{1,0:T(8,128)(2,1)S(1)}, bf16[16,720]{1,0:T(8,128)(2,1)S(1)}, u32[]{:S(2)}, u32[]{:S(2)}) %collective-permute-start.5) | collective-permute-done | bytes 23072 | tf_op jit(solution)/shard_map/ppermute | solution.py:185
  (97 shorter events, 11.5 us)
Async XLA Ops:
  0.0 7.9 %copy-start = (bf16[16,1,64,512]{3,2,1,0:T(8,128)(2,1)S(1)}, bf16[16,1,64,512]{3,2,1,0:T(8,128)(2,1)}, u32[]{:S(2)}) copy-start(bf16[16,1,64,512]{3,2,1,0:T(8,128)(2,1)} %param.19) | copy-start | bytes 3145732
  0.0 7.6 %copy-start.1 = (bf16[16,512]{1,0:T(8,128)(2,1)S(1)}, bf16[16,512]{1,0:T(8,128)(2,1)}, u32[]{:S(2)}) copy-start(bf16[16,512]{1,0:T(8,128)(2,1)} %param.18) | copy-start | bytes 49156
  0.0 7.7 %copy-start.7 = (s32[16]{0:T(128)S(1)}, s32[16]{0:T(128)}, u32[]{:S(2)}) copy-start(s32[16]{0:T(128)} %param.23) | copy-start | bytes 196
  0.0 7.8 %copy-start.12 = (bf16[16,64]{1,0:T(8,128)(2,1)S(1)}, bf16[16,64]{1,0:T(8,128)(2,1)}, u32[]{:S(2)}) copy-start(bf16[16,64]{1,0:T(8,128)(2,1)} %param.21) | copy-start | bytes 6148
  1.6 8.7 %all-to-all-start.1 = ((bf16[4,45,512]{2,1,0:T(8,128)(2,1)}), bf16[4,45,512]{2,1,0:T(8,128)(2,1)S(1)}, u32[]{:S(2)}, u32[]{:S(2)}) async-start(bf16[4,45,512]{2,1,0:T(8,128)(2,1)} %broadcast_in_dim.99), calls=%async_computation.1 | async-start | bytes 393216 | tf_op jit(solution)/shard_map/all_to_all | solution.py:49
  5.8 2.5 %copy-start.6 = (f32[8]{0:T(128)S(1)}, f32[8]{0:T(128)}, u32[]{:S(2)}) copy-start(f32[8]{0:T(128)} %param.24) | copy-start | bytes 100
  7.5 1.2 copy-start.8
  10.3 35.8 %all-to-all-start = ((bf16[16,16,640]{2,1,0:T(8,128)(2,1)}), bf16[16,16,640]{2,1,0:T(8,128)(2,1)S(1)}, u32[]{:S(2)}, u32[]{:S(2)}) async-start(bf16[16,16,640]{2,1,0:T(8,128)(2,1)} %maximum_maximum_fusion), calls=%async_computation | async-start | bytes 655360 | tf_op jit(solution)/shard_map/all_to_all | solution.py:49
  47.4 15.7 %all-to-all-start.2 = ((bf16[8,64,180]{2,1,0:T(8,128)(2,1)}), bf16[8,64,180]{2,1,0:T(8,128)(2,1)S(1)}, u32[]{:S(2)}, u32[]{:S(2)}) async-start(bf16[8,64,180]{2,1,0:T(8,128)(2,1)} %bitcast.9), calls=%async_computation.2 | async-start | bytes 524288 | tf_op jit(solution)/shard_map/all_to_all | solution.py:49
  83.6 6.5 %copy-start.2 = (bf16[32,180]{1,0:T(8,128)(2,1)S(1)}, bf16[32,180]{1,0:T(8,128)(2,1)}, u32[]{:S(2)}) copy-start(bf16[32,180]{1,0:T(8,128)(2,1)} %param.34) | copy-start | bytes 34564
  83.6 10.9 %copy-start.3 = (bf16[32,180]{1,0:T(8,128)(2,1)S(1)}, bf16[32,180]{1,0:T(8,128)(2,1)}, u32[]{:S(2)}) copy-start(bf16[32,180]{1,0:T(8,128)(2,1)} %param.35) | copy-start | bytes 34564
  84.5 14.6 %copy-start.9 = (bf16[2880,32]{0,1:T(8,128)(2,1)S(1)}, bf16[2880,32]{0,1:T(8,128)(2,1)}, u32[]{:S(2)}) copy-start(bf16[2880,32]{0,1:T(8,128)(2,1)} %param.33) | copy-start | bytes 552964
  84.5 14.6 %copy-start.11 = (f32[2880]{0:T(1024)S(1)}, f32[2880]{0:T(1024)}, u32[]{:S(2)}) copy-start(f32[2880]{0:T(1024)} %param.27) | copy-start | bytes 34564
  84.5 14.3 %all-to-all-start.4 = ((bf16[8,16,2884]{2,1,0:T(8,128)(2,1)}), bf16[8,16,2884]{2,1,0:T(8,128)(2,1)S(1)}, u32[]{:S(2)}, u32[]{:S(2)}) async-start(bf16[8,16,2884]{2,1,0:T(8,128)(2,1)} %broadcast_in_dim.104), calls=%async_computation.4 | async-start | bytes 1507328 | tf_op jit(solution)/shard_map/all_to_all | solution.py:49
  88.2 14.5 %collective-permute-start.4 = (bf16[180,2880]{1,0:T(8,128)(2,1)}, bf16[180,2880]{1,0:T(8,128)(2,1)}, u32[]{:S(2)}, u32[]{:S(2)}) collective-permute-start(bf16[180,2880]{1,0:T(8,128)(2,1)} %param.32), channel_id=1, source_target_pairs={{0,4},{4,0},{1,5},{5,1},{2,6},{6,2},{3,7},{7,3},{8,12},{12,8},{9,1... | collective-permute-start | bytes 3110408 | tf_op jit(solution)/shard_map/ppermute | solution.py:106
  90.1 9.4 %collective-permute-start.3 = (bf16[32,180]{1,0:T(8,128)(2,1)S(1)}, bf16[32,180]{1,0:T(8,128)(2,1)S(1)}, u32[]{:S(2)}, u32[]{:S(2)}) collective-permute-start(bf16[32,180]{1,0:T(8,128)(2,1)S(1)} %copy-done.2), channel_id=1, source_target_pairs={{0,4},{4,0},{1,5},{5,1},{2,6},{6,2},{3,7},{7,3},{8,12},{12,8},{9,1... | collective-permute-start | bytes 34568 | tf_op jit(solution)/shard_map/ppermute | solution.py:107
  92.6 7.7 %collective-permute-start.2 = (bf16[180,2880]{1,0:T(8,128)(2,1)}, bf16[180,2880]{1,0:T(8,128)(2,1)}, u32[]{:S(2)}, u32[]{:S(2)}) collective-permute-start(bf16[180,2880]{1,0:T(8,128)(2,1)} %bitcast.22), channel_id=1, source_target_pairs={{0,4},{4,0},{1,5},{5,1},{2,6},{6,2},{3,7},{7,3},{8,12},{12,8},{9,1... | collective-permute-start | bytes 3110408 | tf_op jit(solution)/shard_map/ppermute | solution.py:104
  94.5 5.4 %collective-permute-start.1 = (bf16[32,180]{1,0:T(8,128)(2,1)S(1)}, bf16[32,180]{1,0:T(8,128)(2,1)S(1)}, u32[]{:S(2)}, u32[]{:S(2)}) collective-permute-start(bf16[32,180]{1,0:T(8,128)(2,1)S(1)} %copy-done.3), channel_id=1, source_target_pairs={{0,4},{4,0},{1,5},{5,1},{2,6},{6,2},{3,7},{7,3},{8,12},{12,8},{9,1... | collective-permute-start | bytes 34568 | tf_op jit(solution)/shard_map/ppermute | solution.py:108
  96.9 5.8 %collective-permute-start = (bf16[180,2880]{1,0:T(8,128)(2,1)}, bf16[180,2880]{1,0:T(8,128)(2,1)}, u32[]{:S(2)}, u32[]{:S(2)}) collective-permute-start(bf16[180,2880]{1,0:T(8,128)(2,1)} %bitcast.21), channel_id=1, source_target_pairs={{0,4},{4,0},{1,5},{5,1},{2,6},{6,2},{3,7},{7,3},{8,12},{12,8},{9,1... | collective-permute-start | bytes 3110408 | tf_op jit(solution)/shard_map/ppermute | solution.py:105
  109.0 6.0 %copy-start.10 = (bf16[2880,32]{0,1:T(8,128)(2,1)S(1)}, bf16[2880,32]{0,1:T(8,128)(2,1)}, u32[]{:S(2)}) copy-start(bf16[2880,32]{0,1:T(8,128)(2,1)} %param.28) | copy-start | bytes 552964
  109.0 19.3 %all-to-all-start.5 = ((bf16[8,64,720]{2,1,0:T(8,128)(2,1)}), bf16[8,64,720]{2,1,0:T(8,128)(2,1)S(1)}, u32[]{:S(2)}, u32[]{:S(2)}) async-start(bf16[8,64,720]{2,1,0:T(8,128)(2,1)} %bitcast.24), calls=%async_computation.5 | async-start | bytes 1572864 | tf_op jit(solution)/shard_map/all_to_all | solution.py:49
  115.5 18.4 %copy-start.4 = (s32[16,4]{0,1:T(4,128)S(1)}, s32[16,4]{0,1:T(4,128)}, u32[]{:S(2)}) copy-start(s32[16,4]{0,1:T(4,128)} %param.29) | copy-start | bytes 772
  129.2 17.9 %all-to-all-start.6 = ((bf16[16,4,720]{2,1,0:T(4,128)(2,1)}), bf16[16,4,720]{2,1,0:T(4,128)(2,1)S(1)}, u32[]{:S(2)}, u32[]{:S(2)}) async-start(bf16[16,4,720]{2,1,0:T(4,128)(2,1)} %reshape.198), calls=%async_computation.6 | async-start | bytes 196608 | tf_op jit(solution)/shard_map/all_to_all | solution.py:49
  147.3 7.2 %collective-permute-start.5 = (bf16[16,720]{1,0:T(8,128)(2,1)S(1)}, bf16[16,720]{1,0:T(8,128)(2,1)S(1)}, u32[]{:S(2)}, u32[]{:S(2)}) collective-permute-start(bf16[16,720]{1,0:T(8,128)(2,1)S(1)} %fusion.34), channel_id=1, source_target_pairs={{0,256},{256,0},{1,257},{257,1},{2,258},{258,2},{3,259},{259,3},{4... | collective-permute-start | bytes 69128 | tf_op jit(solution)/shard_map/ppermute | solution.py:185
  (1 other events, 1.0 us)

commit v2 on v1

--- a/solution.py
+++ b/solution.py
@@ -1,8 +1,11 @@
+import functools
 import math
 
 import jax
 import jax.numpy as jnp
 from jax import lax
+from jax.experimental import pallas as pl
+from jax.experimental.pallas import tpu as pltpu
 from jax.sharding import Mesh, PartitionSpec as P
 
 CAP = 4
@@ -61,6 +64,82 @@
     ).astype(jnp.int32)
     slots = lax.broadcasted_iota(jnp.int32, (1, 1, CAP, 1), 2)
     return (member[:, :, None, :] & (before[:, :, None, :] == slots)).astype(BF16)
+
+
+def expert_kernel(n_ylo, n_cuts, topk, *refs):
+    (expert_ref, rows_ref, gain_ref, router_ref, low_ref, *rest) = refs
+    adapters, weights = rest[:2], rest[2:8]
+    out_ref, held, sems = rest[8:]
+    copies = [
+        pltpu.make_async_copy(weights[i], held.at[i], sems.at[i]) for i in range(len(weights))
+    ]
+    for copy in copies:
+        copy.start()
+    width = gain_ref.shape[1]
+    quarter = width // n_cuts
+    nt = (((1,), (1,)), ((), ()))
+    middle = rows_ref[:, :width].astype(F32)
+    inverse = lax.rsqrt(jnp.mean(middle * middle, axis=1, keepdims=True) + EPSILON)
+    normed = (middle * inverse * gain_ref[...]).astype(BF16)
+    raw = jax.nn.sigmoid(lax.dot_general(normed, router_ref[...], nt, preferred_element_type=F32))
+    names = lax.broadcasted_iota(jnp.int32, raw.shape, 1)
+    named = names < 0
+    for entry in range(topk):
+        route = rows_ref[:, width + entry : width + entry + 1].astype(F32).astype(jnp.int32)
+        named = named | (names == route)
+    own = jnp.sum(jnp.where(names == expert_ref[0], raw, 0.0), axis=1, keepdims=True)
+    row_weight = own / jnp.sum(jnp.where(named, raw, 0.0), axis=1, keepdims=True)
+    low_code = lax.dot_general(normed, low_ref[...], nt, preferred_element_type=F32).astype(BF16)
+    rank = low_ref.shape[0]
+    total = None
+    for half in range(2):
+        copies[3 * half].wait()
+        pre_gate = lax.dot_general(normed, held[3 * half], nt, preferred_element_type=F32)
+        pre_gate = pre_gate + jnp.dot(
+            low_code, adapters[half][:rank], preferred_element_type=F32
+        )
+        copies[3 * half + 1].wait()
+        pre_up = lax.dot_general(normed, held[3 * half + 1], nt, preferred_element_type=F32)
+        pre_up = pre_up + jnp.dot(low_code, adapters[half][rank:], preferred_element_type=F32)
+        activated = (pre_up + 1.0) * pre_gate * jax.nn.sigmoid(1.702 * pre_gate)
+        copies[3 * half + 2].wait()
+        part = jnp.dot(activated.astype(BF16), held[3 * half + 2], preferred_element_type=F32)
+        total = part if total is None else total + part
+    total = total * row_weight
+    own_rows = total.shape[0] // n_ylo
+    for peer in range(n_ylo * n_cuts):
+        row, column = peer // n_cuts * own_rows, peer % n_cuts * quarter
+        out_ref[peer] = total[row : row + own_rows, column : column + quarter].astype(BF16)
+
+
+def expert_rows(row_block, own, other, norm_gain, router, adapter_in, expert, counts):
+    n_ylo, n_cuts, topk = counts
+    width = norm_gain.shape[0]
+    rows = row_block.shape[0]
+    whole = pl.BlockSpec(memory_space=pltpu.VMEM)
+    weights = own[:3] + other[:3]
+    return pl.pallas_call(
+        functools.partial(expert_kernel, n_ylo, n_cuts, topk),
+        out_shape=jax.ShapeDtypeStruct((n_ylo * n_cuts, rows // n_ylo, width // n_cuts), BF16),
+        in_specs=[pl.BlockSpec(memory_space=pltpu.SMEM)]
+        + [whole] * 6
+        + [pl.BlockSpec(memory_space=pl.ANY)] * len(weights),
+        out_specs=whole,
+        scratch_shapes=[
+            pltpu.VMEM((len(weights),) + weights[0].shape, BF16),
+            pltpu.SemaphoreType.DMA((len(weights),)),
+        ],
+        name="expert_rows",
+    )(
+        expert.reshape(1).astype(jnp.int32),
+        row_block,
+        norm_gain[None],
+        router.T,
+        adapter_in.T,
+        own[3],
+        other[3],
+        *weights,
+    )
 
 
 def shards(
@@ -98,14 +177,17 @@
     quarter = width // n_cuts
     swap = [(0, 1), (1, 0)]
 
-    plane_proj = exchange(
-        jnp.broadcast_to(attn_proj.T[None], (4, piece, heads_in)), ("ylo", "core")
-    ).reshape(strip, heads_in)
-    gate_t = jnp.concatenate([expert_gate.T, lax.ppermute(expert_gate.T, "core", swap)], 0)
-    up_t = jnp.concatenate([expert_up.T, lax.ppermute(expert_up.T, "core", swap)], 0)
-    down = jnp.concatenate([expert_down, lax.ppermute(expert_down, "core", swap)], 0)
-    adapt_gate = jnp.concatenate([adapter_gate, lax.ppermute(adapter_gate, "core", swap)], 1)
-    adapt_up = jnp.concatenate([adapter_up, lax.ppermute(adapter_up, "core", swap)], 1)
+    pieces = [attn_proj.T]
+    for axes in ("core", "ylo", ("ylo", "core")):
+        flip = swap if isinstance(axes, str) else [(i, 3 - i) for i in range(4)]
+        pieces.append(lax.ppermute(attn_proj.T, axes, flip))
+    core = lax.axis_index("core")
+    pieces = [jnp.where(core == 0, pieces[i], pieces[i ^ 1]) for i in range(4)]
+    pieces = [jnp.where(ylo == 0, pieces[i], pieces[i ^ 2]) for i in range(4)]
+    plane_proj = jnp.concatenate(pieces, 0)
+    adapters = jnp.concatenate([adapter_gate, adapter_up], 0)
+    hidden_own = (expert_gate.T, expert_up.T, expert_down, adapters)
+    hidden_other = tuple(lax.ppermute(part, "core", swap) for part in hidden_own)
 
     attn_out = attention_rows(
         queries, cache_keys, cache_values, new_keys, new_values, lengths, head_sinks
@@ -122,7 +204,8 @@
         ],
         axis=2,
     )
-    held = exchange(payload, "z").reshape(planes * rows, heads_in + 128)
+    held = exchange(payload, "z")
+    held = held.reshape(planes * rows, heads_in + 128)
     line = lax.broadcasted_iota(jnp.int32, (strip, 128), 1)
     column = lax.broadcasted_iota(jnp.int32, (strip, 128), 0)
     residual_part = jnp.where((column == cut * piece + line) & (line < piece), 1.0 / n_side, 0.0)
@@ -143,47 +226,37 @@
     outgoing = outgoing.reshape(planes, blocks * CAP, strip + topk)
     arrived = exchange(outgoing, "z")
     row_part = arrived[:, :, :strip].transpose(1, 0, 2).reshape(blocks * CAP, width)
-    row_part = jnp.concatenate([row_part, arrived[0, :, strip:]], 1)
+    lanes = -(-(width + topk) // 128) * 128
+    spare = jnp.zeros((blocks * CAP, lanes - width - topk), BF16)
+    row_part = jnp.concatenate([row_part, arrived[0, :, strip:], spare], 1)
     peers = n_ylo * n_cuts
     row_block = exchange(jnp.broadcast_to(row_part[None], (peers,) + row_part.shape), ("ylo", "cuts"))
-    row_block = row_block.reshape(-1, width + topk)
-
-    middle_rows = row_block[:, :width].astype(F32)
-    row_routes = row_block[:, width:].astype(jnp.int32)
-    inverse = lax.rsqrt(jnp.mean(middle_rows * middle_rows, axis=1, keepdims=True) + EPSILON)
-    normed = (middle_rows * inverse * norm_gain).astype(BF16)
-    raw = jax.nn.sigmoid(jnp.dot(normed, router, preferred_element_type=F32))
+    row_block = row_block.reshape(-1, lanes)
+
     expert = side * planes + plane
-    names = lax.broadcasted_iota(jnp.int32, (1, router.shape[1]), 1)
-    named = jnp.any(row_routes[:, :, None] == names[:, None, :], axis=1)
-    row_weight = jnp.sum(jnp.where(names == expert, raw, 0.0), axis=1) / jnp.sum(
-        jnp.where(named, raw, 0.0), axis=1
-    )
-    first = (row_routes[:, 0] == expert).astype(F32)
-    low_code = jnp.dot(normed, adapter_in, preferred_element_type=F32).astype(BF16)
-    nt = (((1,), (1,)), ((), ()))
-    pre_gate = lax.dot_general(normed, gate_t, nt, preferred_element_type=F32)
-    pre_gate = pre_gate + jnp.dot(low_code, adapt_gate, preferred_element_type=F32)
-    pre_up = lax.dot_general(normed, up_t, nt, preferred_element_type=F32)
-    pre_up = pre_up + jnp.dot(low_code, adapt_up, preferred_element_type=F32)
-    activated = ((pre_up + 1.0) * pre_gate * jax.nn.sigmoid(1.702 * pre_gate)).astype(BF16)
-    value = jnp.dot(activated, down, preferred_element_type=F32).astype(BF16)
-
-    own_rows = value.shape[0] // n_ylo
-    value = value.reshape(n_ylo, own_rows, n_cuts, quarter).transpose(0, 2, 1, 3)
-    value = exchange(value.reshape(peers, own_rows, quarter), ("ylo", "cuts"))
+    value = expert_rows(
+        row_block,
+        hidden_own,
+        hidden_other,
+        norm_gain,
+        router,
+        adapter_in,
+        expert,
+        (n_ylo, n_cuts, topk),
+    )
+
+    own_rows = row_block.shape[0] // n_ylo
+    value = exchange(value, ("ylo", "cuts"))
     total = jnp.sum(value.astype(F32), axis=0)
-    own_weight = lax.dynamic_slice_in_dim(row_weight, ylo * own_rows, own_rows)
-    own_first = lax.dynamic_slice_in_dim(first, ylo * own_rows, own_rows)
-    own_middle = lax.dynamic_slice(
-        row_block, (ylo * own_rows, cut * quarter), (own_rows, quarter)
-    ).astype(F32)
-    total = (total * own_weight[:, None] + own_middle * own_first[:, None]).astype(BF16)
-    returned = exchange(total.reshape(planes, CAP, quarter), "z")
-    own_hot = slot_hot(expert_routes[None], experts)[:, 0]
-    out = jnp.einsum("ztr,ztd->rd", own_hot, returned, preferred_element_type=F32).astype(BF16)
-    other = lax.ppermute(out, "side", swap)
-    return (out.astype(F32) + other.astype(F32)).astype(BF16)
+    mine = lax.dynamic_slice_in_dim(row_block, ylo * own_rows, own_rows)
+    first = (mine[:, width].astype(jnp.int32) == expert).astype(F32)
+    own_middle = lax.dynamic_slice_in_dim(mine, cut * quarter, quarter, 1).astype(F32)
+    total = (total + own_middle * first[:, None]).astype(BF16)
+    total = jnp.broadcast_to(total.reshape(1, planes, CAP, quarter), (n_side, planes, CAP, quarter))
+    returned = exchange(total.reshape(n_side * planes, CAP, quarter), ("side", "z"))
+    own_hot = slot_hot(expert_routes[None], jnp.arange(n_side * planes))[:, 0]
+    out = jnp.einsum("etr,etd->rd", own_hot, returned, preferred_element_type=F32)
+    return out.astype(BF16)
 
 
 def solution(mesh):
@@ -211,6 +284,7 @@
         P(None, hidden),
         P(None, hidden),
     )
+
     return jax.shard_map(
         shards, mesh=fine, in_specs=placed, out_specs=P(group, "cuts"), check_vma=False
     )

time: 156 us -> 152 us (0.974)
  the two profiles are of different devices: /device:TPU:32 before, /device:TPU:8 now
where the time goes in v2:
time: 152 us; the launch traced here: 151 us
  starting transfers between devices  64.1 us (42%)
  waiting for transfers between devices  63.5 us (42%)
  Pallas kernels  8.08 us (5%)
  local copies, waits for them, and re-layouts  7.4 us (5%)
  other arithmetic  4.24 us (3%)
  matrix products  3.27 us (2%)
    all_to_all x6, waiting for transfers between devices, exchange(): return lax.all_to_all(array, axes, split_axis=0, concat_axis=0, tiled=True)  60.8 us
    all_to_all x6, starting transfers between devices, exchange(): return lax.all_to_all(array, axes, split_axis=0, concat_axis=0, tiled=True)  48.3 us
    ppermute x4, starting transfers between devices, shards(): lax.ppermute(part, 'core', swap)  8.18 us
    pallas_call x1, Pallas kernels, expert_rows(): pl.pallas_call(functools.partial(expert_kernel, n_ylo, n_cuts, topk), out...  8.08 us
    ppermute x3, starting transfers between devices, shards(): pieces.append(lax.ppermute(attn_proj.T, axes, flip))  7.59 us
  transfers between devices with their start and end apart: 13, of which 9 were waited for; matrix products, arithmetic and copies ran while one was open for 2% of the time, Pallas kernels for 0%

profile of v2, /device:TPU:8, one launch (start us, length us, event | category | flops | bytes accessed | tf_op | source)
XLA Modules:
  0.0 151.1 jit_solution(18375567937814539308)
XLA Ops:
  5.8 15.2 %all-to-all-start = ((bf16[16,16,640]{2,1,0:T(8,128)(2,1)}), bf16[16,16,640]{2,1,0:T(8,128)(2,1)S(1)}, u32[]{:S(2)}, u32[]{:S(2)}) async-start(bf16[16,16,640]{2,1,0:T(8,128)(2,1)} %maximum_maximum_fusion), calls=%async_computation | async-start | bytes 655360 | tf_op jit(solution)/shard_map/all_to_all | solution.py:52
  21.0 1.9 %collective-permute-start = (bf16[45,512]{1,0:T(8,128)(2,1)S(1)}, bf16[45,512]{1,0:T(8,128)(2,1)S(1)}, u32[]{:S(2)}, u32[]{:S(2)}) collective-permute-start(bf16[45,512]{1,0:T(8,128)(2,1)S(1)} %bitcast.75), channel_id=1, source_target_pairs={{0,4},{4,0},{1,5},{5,1},{2,6},{6,2},{3,7},{7,3},{8,12},{12,8},{9,1... | collective-permute-start | bytes 138248 | tf_op jit(solution)/shard_map/ppermute | solution.py:183
  22.9 2.4 %collective-permute-start.1 = (bf16[45,512]{1,0:T(8,128)(2,1)S(1)}, bf16[45,512]{1,0:T(8,128)(2,1)S(1)}, u32[]{:S(2)}, u32[]{:S(2)}) collective-permute-start(bf16[45,512]{1,0:T(8,128)(2,1)S(1)} %bitcast.76), channel_id=1, source_target_pairs={{0,8},{8,0},{1,9},{9,1},{2,10},{10,2},{3,11},{11,3},{4,12},{12,4},... | collective-permute-start | bytes 138248 | tf_op jit(solution)/shard_map/ppermute | solution.py:183
  25.3 3.3 %collective-permute-start.2 = (bf16[45,512]{1,0:T(8,128)(2,1)S(1)}, bf16[45,512]{1,0:T(8,128)(2,1)S(1)}, u32[]{:S(2)}, u32[]{:S(2)}) collective-permute-start(bf16[45,512]{1,0:T(8,128)(2,1)S(1)} %bitcast.77), channel_id=1, source_target_pairs={{0,12},{4,8},{8,4},{12,0},{1,13},{5,9},{9,5},{13,1},{2,14},{6,10},... | collective-permute-start | bytes 138248 | tf_op jit(solution)/shard_map/ppermute | solution.py:183
  28.9 1.9 %collective-permute-done.2 = bf16[45,512]{1,0:T(8,128)(2,1)S(1)} collective-permute-done((bf16[45,512]{1,0:T(8,128)(2,1)S(1)}, bf16[45,512]{1,0:T(8,128)(2,1)S(1)}, u32[]{:S(2)}, u32[]{:S(2)}) %collective-permute-start.2) | collective-permute-done | bytes 46112 | tf_op jit(solution)/shard_map/ppermute | solution.py:183
  30.8 11.0 %all-to-all-done = bf16[16,16,640]{2,1,0:T(8,128)(2,1)S(1)} async-done(((bf16[16,16,640]{2,1,0:T(8,128)(2,1)}), bf16[16,16,640]{2,1,0:T(8,128)(2,1)S(1)}, u32[]{:S(2)}, u32[]{:S(2)}) %all-to-all-start) | async-done | bytes 327712 | tf_op jit(solution)/shard_map/all_to_all | solution.py:52
  43.1 6.0 %all-to-all-start.1 = ((bf16[8,64,180]{2,1,0:T(8,128)(2,1)}), bf16[8,64,180]{2,1,0:T(8,128)(2,1)S(1)}, u32[]{:S(2)}, u32[]{:S(2)}) async-start(bf16[8,64,180]{2,1,0:T(8,128)(2,1)} %bitcast.10), calls=%async_computation.1 | async-start | bytes 524288 | tf_op jit(solution)/shard_map/all_to_all | solution.py:52
  49.4 8.5 %all-to-all-done.1 = bf16[8,64,180]{2,1,0:T(8,128)(2,1)S(1)} async-done(((bf16[8,64,180]{2,1,0:T(8,128)(2,1)}), bf16[8,64,180]{2,1,0:T(8,128)(2,1)S(1)}, u32[]{:S(2)}, u32[]{:S(2)}) %all-to-all-start.1) | async-done | bytes 184352 | tf_op jit(solution)/shard_map/all_to_all | solution.py:52
  58.8 6.1 %all-to-all-start.2 = ((bf16[16,16,184]{2,1,0:T(8,128)(2,1)}), bf16[16,16,184]{2,1,0:T(8,128)(2,1)S(1)}, u32[]{:S(2)}, u32[]{:S(2)}) async-start(bf16[16,16,184]{2,1,0:T(8,128)(2,1)} %copy.54), calls=%async_computation.2 | async-start | bytes 262144 | tf_op jit(solution)/shard_map/all_to_all | solution.py:52
  65.0 1.9 %collective-permute-start.4 = (bf16[180,2880]{1,0:T(8,128)(2,1)S(1)}, bf16[180,2880]{1,0:T(8,128)(2,1)}, u32[]{:S(2)}, u32[]{:S(2)}) collective-permute-start(bf16[180,2880]{1,0:T(8,128)(2,1)S(1)} %bitcast.65), channel_id=1, source_target_pairs={{0,4},{4,0},{1,5},{5,1},{2,6},{6,2},{3,7},{7,3},{8,12},{12,8},{9,1... | collective-permute-start | bytes 3110408 | tf_op jit(solution)/shard_map/ppermute | solution.py:190
  66.9 2.4 %collective-permute-start.5 = (bf16[180,2880]{1,0:T(8,128)(2,1)}, bf16[180,2880]{1,0:T(8,128)(2,1)}, u32[]{:S(2)}, u32[]{:S(2)}) collective-permute-start(bf16[180,2880]{1,0:T(8,128)(2,1)} %bitcast.25.refs_8_), channel_id=1, source_target_pairs={{0,4},{4,0},{1,5},{5,1},{2,6},{6,2},{3,7},{7,3},{8,12},{12,8},{9,1... | collective-permute-start | bytes 3110408 | tf_op jit(solution)/shard_map/ppermute | solution.py:190
  69.3 1.9 %collective-permute-start.6 = (bf16[180,2880]{1,0:T(8,128)(2,1)}, bf16[180,2880]{1,0:T(8,128)(2,1)}, u32[]{:S(2)}, u32[]{:S(2)}) collective-permute-start(bf16[180,2880]{1,0:T(8,128)(2,1)} %refs_9_.1), channel_id=1, source_target_pairs={{0,4},{4,0},{1,5},{5,1},{2,6},{6,2},{3,7},{7,3},{8,12},{12,8},{9,1... | collective-permute-start | bytes 3110408 | tf_op jit(solution)/shard_map/ppermute | solution.py:190
  71.2 7.6 %all-to-all-done.2 = bf16[16,16,184]{2,1,0:T(8,128)(2,1)S(1)} async-done(((bf16[16,16,184]{2,1,0:T(8,128)(2,1)}), bf16[16,16,184]{2,1,0:T(8,128)(2,1)S(1)}, u32[]{:S(2)}, u32[]{:S(2)}) %all-to-all-start.2) | async-done | bytes 94240 | tf_op jit(solution)/shard_map/all_to_all | solution.py:52
  79.3 0.9 broadcast_in_dim.93
  80.2 4.8 %all-to-all-start.3 = ((bf16[8,16,2944]{2,1,0:T(8,128)(2,1)}), bf16[8,16,2944]{2,1,0:T(8,128)(2,1)S(1)}, u32[]{:S(2)}, u32[]{:S(2)}) async-start(bf16[8,16,2944]{2,1,0:T(8,128)(2,1)} %broadcast_in_dim.93), calls=%async_computation.3 | async-start | bytes 1507328 | tf_op jit(solution)/shard_map/all_to_all | solution.py:52
  85.1 1.9 %collective-permute-start.3 = (bf16[64,180]{1,0:T(8,128)(2,1)S(1)}, bf16[64,180]{1,0:T(8,128)(2,1)S(1)}, u32[]{:S(2)}, u32[]{:S(2)}) collective-permute-start(bf16[64,180]{1,0:T(8,128)(2,1)S(1)} %constant_dynamic-update-slice_fusion.refs_5_), channel_id=1, source_target_pairs={{0,4},{4,0},{1,5},{5,1},{2,6},{6,2},{3,7},{7,3},{8,12},{12,8},{9,1... | collective-permute-start | bytes 69128 | tf_op jit(solution)/shard_map/ppermute | solution.py:190
  88.2 5.3 %all-to-all-done.3 = bf16[8,16,2944]{2,1,0:T(8,128)(2,1)S(1)} async-done(((bf16[8,16,2944]{2,1,0:T(8,128)(2,1)}), bf16[8,16,2944]{2,1,0:T(8,128)(2,1)S(1)}, u32[]{:S(2)}, u32[]{:S(2)}) %all-to-all-start.3) | async-done | bytes 753696 | tf_op jit(solution)/shard_map/all_to_all | solution.py:52
  94.4 8.1 %expert_rows.1 = bf16[8,64,720]{2,1,0:T(8,128)(2,1)} custom-call(s32[1]{0:T(128)} %bitcast.refs_0_, bf16[128,2944]{1,0:T(8,128)(2,1)} %bitcast.61, f32[1,2880]{1,0:T(1,128)} %broadcast_in_dim.94.refs_2_, bf16[32,2880]{1,0:T(8,128)(2,1)} %bitcast.71, bf16[32,2880]{1,0:T(8,128)(2,1)} %bitcast.72, bf16[64,180]{1,0:T(8,128)(2,1)} %copy-done.4, ...), custom_call_target="tpu_custom_call" | custom-call | tf_op jit(solution)/shard_map/expert_rows/pallas_call | solution.py:121
  102.5 5.0 %all-to-all-start.4 = ((bf16[8,64,720]{2,1,0:T(8,128)(2,1)}), bf16[8,64,720]{2,1,0:T(8,128)(2,1)S(1)}, u32[]{:S(2)}, u32[]{:S(2)}) async-start(bf16[8,64,720]{2,1,0:T(8,128)(2,1)} %expert_rows.1), calls=%async_computation.4 | async-start | bytes 1572864 | tf_op jit(solution)/shard_map/all_to_all | solution.py:52
  107.4 0.9 convert_reduce_fusion.1
  108.3 7.7 %all-to-all-done.4 = bf16[8,64,720]{2,1,0:T(8,128)(2,1)S(1)} async-done(((bf16[8,64,720]{2,1,0:T(8,128)(2,1)}), bf16[8,64,720]{2,1,0:T(8,128)(2,1)S(1)}, u32[]{:S(2)}, u32[]{:S(2)}) %all-to-all-start.4) | async-done | bytes 737312 | tf_op jit(solution)/shard_map/all_to_all | solution.py:52
  116.2 1.0 add_convert_fusion
  118.0 11.2 %all-to-all-start.5 = ((bf16[32,4,720]{2,1,0:T(4,128)(2,1)}), bf16[32,4,720]{2,1,0:T(4,128)(2,1)S(1)}, u32[]{:S(2)}, u32[]{:S(2)}) async-start(bf16[32,4,720]{2,1,0:T(4,128)(2,1)} %bitcast.26), calls=%async_computation.5 | async-start | bytes 393216 | tf_op jit(solution)/shard_map/all_to_all | solution.py:52
  129.5 20.8 %all-to-all-done.5 = bf16[32,4,720]{2,1,0:T(4,128)(2,1)S(1)} async-done(((bf16[32,4,720]{2,1,0:T(4,128)(2,1)}), bf16[32,4,720]{2,1,0:T(4,128)(2,1)S(1)}, u32[]{:S(2)}, u32[]{:S(2)}) %all-to-all-start.5) | async-done | bytes 184352 | tf_op jit(solution)/shard_map/all_to_all | solution.py:52
  (85 shorter events, 12.9 us)
Async XLA Ops:
  0.0 2.5 %copy-start = (bf16[16,1,64,512]{3,2,1,0:T(8,128)(2,1)S(1)}, bf16[16,1,64,512]{3,2,1,0:T(8,128)(2,1)}, u32[]{:S(2)}) copy-start(bf16[16,1,64,512]{3,2,1,0:T(8,128)(2,1)} %param.19) | copy-start | bytes 3145732
  0.0 2.9 %copy-start.12 = (f32[8]{0:T(128)S(1)}, f32[8]{0:T(128)}, u32[]{:S(2)}) copy-start(f32[8]{0:T(128)} %param.24) | copy-start | bytes 100
  0.0 3.1 %copy-start.11 = (bf16[16,64]{1,0:T(8,128)(2,1)S(1)}, bf16[16,64]{1,0:T(8,128)(2,1)}, u32[]{:S(2)}) copy-start(bf16[16,64]{1,0:T(8,128)(2,1)} %param.22) | copy-start | bytes 6148
  0.0 3.1 %copy-start.13 = (bf16[16,1,64,512]{3,2,1,0:T(8,128)(2,1)S(1)}, bf16[16,1,64,512]{3,2,1,0:T(8,128)(2,1)}, u32[]{:S(2)}) copy-start(bf16[16,1,64,512]{3,2,1,0:T(8,128)(2,1)} %param.20) | copy-start | bytes 3145732
  4.5 16.5 %copy-start.5 = (bf16[512,45]{0,1:T(8,128)(2,1)S(1)}, bf16[512,45]{0,1:T(8,128)(2,1)}, u32[]{:S(2)}) copy-start(bf16[512,45]{0,1:T(8,128)(2,1)} %param.25) | copy-start | bytes 138244
  5.8 36.1 %all-to-all-start = ((bf16[16,16,640]{2,1,0:T(8,128)(2,1)}), bf16[16,16,640]{2,1,0:T(8,128)(2,1)S(1)}, u32[]{:S(2)}, u32[]{:S(2)}) async-start(bf16[16,16,640]{2,1,0:T(8,128)(2,1)} %maximum_maximum_fusion), calls=%async_computation | async-start | bytes 655360 | tf_op jit(solution)/shard_map/all_to_all | solution.py:52
  21.0 7.7 %collective-permute-start = (bf16[45,512]{1,0:T(8,128)(2,1)S(1)}, bf16[45,512]{1,0:T(8,128)(2,1)S(1)}, u32[]{:S(2)}, u32[]{:S(2)}) collective-permute-start(bf16[45,512]{1,0:T(8,128)(2,1)S(1)} %bitcast.75), channel_id=1, source_target_pairs={{0,4},{4,0},{1,5},{5,1},{2,6},{6,2},{3,7},{7,3},{8,12},{12,8},{9,1... | collective-permute-start | bytes 138248 | tf_op jit(solution)/shard_map/ppermute | solution.py:183
  22.9 6.0 %collective-permute-start.1 = (bf16[45,512]{1,0:T(8,128)(2,1)S(1)}, bf16[45,512]{1,0:T(8,128)(2,1)S(1)}, u32[]{:S(2)}, u32[]{:S(2)}) collective-permute-start(bf16[45,512]{1,0:T(8,128)(2,1)S(1)} %bitcast.76), channel_id=1, source_target_pairs={{0,8},{8,0},{1,9},{9,1},{2,10},{10,2},{3,11},{11,3},{4,12},{12,4},... | collective-permute-start | bytes 138248 | tf_op jit(solution)/shard_map/ppermute | solution.py:183
  25.3 5.5 %collective-permute-start.2 = (bf16[45,512]{1,0:T(8,128)(2,1)S(1)}, bf16[45,512]{1,0:T(8,128)(2,1)S(1)}, u32[]{:S(2)}, u32[]{:S(2)}) collective-permute-start(bf16[45,512]{1,0:T(8,128)(2,1)S(1)} %bitcast.77), channel_id=1, source_target_pairs={{0,12},{4,8},{8,4},{12,0},{1,13},{5,9},{9,5},{13,1},{2,14},{6,10},... | collective-permute-start | bytes 138248 | tf_op jit(solution)/shard_map/ppermute | solution.py:183
  42.3 22.6 %copy-start.2 = (bf16[2880,180]{0,1:T(8,128)(2,1)S(1)}, bf16[2880,180]{0,1:T(8,128)(2,1)}, u32[]{:S(2)}) copy-start(bf16[2880,180]{0,1:T(8,128)(2,1)} %param.30) | copy-start | bytes 3110404
  43.1 14.8 %all-to-all-start.1 = ((bf16[8,64,180]{2,1,0:T(8,128)(2,1)}), bf16[8,64,180]{2,1,0:T(8,128)(2,1)S(1)}, u32[]{:S(2)}, u32[]{:S(2)}) async-start(bf16[8,64,180]{2,1,0:T(8,128)(2,1)} %bitcast.10), calls=%async_computation.1 | async-start | bytes 524288 | tf_op jit(solution)/shard_map/all_to_all | solution.py:52
  58.8 20.0 %all-to-all-start.2 = ((bf16[16,16,184]{2,1,0:T(8,128)(2,1)}), bf16[16,16,184]{2,1,0:T(8,128)(2,1)S(1)}, u32[]{:S(2)}, u32[]{:S(2)}) async-start(bf16[16,16,184]{2,1,0:T(8,128)(2,1)} %copy.54), calls=%async_computation.2 | async-start | bytes 262144 | tf_op jit(solution)/shard_map/all_to_all | solution.py:52
  65.0 23.2 %collective-permute-start.4 = (bf16[180,2880]{1,0:T(8,128)(2,1)S(1)}, bf16[180,2880]{1,0:T(8,128)(2,1)}, u32[]{:S(2)}, u32[]{:S(2)}) collective-permute-start(bf16[180,2880]{1,0:T(8,128)(2,1)S(1)} %bitcast.65), channel_id=1, source_target_pairs={{0,4},{4,0},{1,5},{5,1},{2,6},{6,2},{3,7},{7,3},{8,12},{12,8},{9,1... | collective-permute-start | bytes 3110408 | tf_op jit(solution)/shard_map/ppermute | solution.py:190
  66.9 21.3 %collective-permute-start.5 = (bf16[180,2880]{1,0:T(8,128)(2,1)}, bf16[180,2880]{1,0:T(8,128)(2,1)}, u32[]{:S(2)}, u32[]{:S(2)}) collective-permute-start(bf16[180,2880]{1,0:T(8,128)(2,1)} %bitcast.25.refs_8_), channel_id=1, source_target_pairs={{0,4},{4,0},{1,5},{5,1},{2,6},{6,2},{3,7},{7,3},{8,12},{12,8},{9,1... | collective-permute-start | bytes 3110408 | tf_op jit(solution)/shard_map/ppermute | solution.py:190
  69.3 18.9 %collective-permute-start.6 = (bf16[180,2880]{1,0:T(8,128)(2,1)}, bf16[180,2880]{1,0:T(8,128)(2,1)}, u32[]{:S(2)}, u32[]{:S(2)}) collective-permute-start(bf16[180,2880]{1,0:T(8,128)(2,1)} %refs_9_.1), channel_id=1, source_target_pairs={{0,4},{4,0},{1,5},{5,1},{2,6},{6,2},{3,7},{7,3},{8,12},{12,8},{9,1... | collective-permute-start | bytes 3110408 | tf_op jit(solution)/shard_map/ppermute | solution.py:190
  79.3 5.8 %copy-start.7 = (bf16[32,180]{1,0:T(8,128)(2,1)S(1)}, bf16[32,180]{1,0:T(8,128)(2,1)}, u32[]{:S(2)}) copy-start(bf16[32,180]{1,0:T(8,128)(2,1)} %param.34) | copy-start | bytes 34564
  79.3 5.8 %copy-start.8 = (bf16[32,180]{1,0:T(8,128)(2,1)S(1)}, bf16[32,180]{1,0:T(8,128)(2,1)}, u32[]{:S(2)}) copy-start(bf16[32,180]{1,0:T(8,128)(2,1)} %param.35) | copy-start | bytes 34564
  79.3 7.7 %copy-start.9 = (f32[2880]{0:T(1024)S(1)}, f32[2880]{0:T(1024)}, u32[]{:S(2)}) copy-start(f32[2880]{0:T(1024)} %param.27) | copy-start | bytes 34564
  80.2 13.3 %all-to-all-start.3 = ((bf16[8,16,2944]{2,1,0:T(8,128)(2,1)}), bf16[8,16,2944]{2,1,0:T(8,128)(2,1)S(1)}, u32[]{:S(2)}, u32[]{:S(2)}) async-start(bf16[8,16,2944]{2,1,0:T(8,128)(2,1)} %broadcast_in_dim.93), calls=%async_computation.3 | async-start | bytes 1507328 | tf_op jit(solution)/shard_map/all_to_all | solution.py:52
  85.1 8.4 %copy-start.4 = (bf16[64,180]{1,0:T(8,128)(2,1)}, bf16[64,180]{1,0:T(8,128)(2,1)S(1)}, u32[]{:S(2)}) copy-start(bf16[64,180]{1,0:T(8,128)(2,1)S(1)} %constant_dynamic-update-slice_fusion.refs_5_) | copy-start | bytes 69124
  85.1 3.1 %collective-permute-start.3 = (bf16[64,180]{1,0:T(8,128)(2,1)S(1)}, bf16[64,180]{1,0:T(8,128)(2,1)S(1)}, u32[]{:S(2)}, u32[]{:S(2)}) collective-permute-start(bf16[64,180]{1,0:T(8,128)(2,1)S(1)} %constant_dynamic-update-slice_fusion.refs_5_), channel_id=1, source_target_pairs={{0,4},{4,0},{1,5},{5,1},{2,6},{6,2},{3,7},{7,3},{8,12},{12,8},{9,1... | collective-permute-start | bytes 69128 | tf_op jit(solution)/shard_map/ppermute | solution.py:190
  88.2 5.3 %copy-start.6 = (bf16[64,180]{1,0:T(8,128)(2,1)}, bf16[64,180]{1,0:T(8,128)(2,1)S(1)}, u32[]{:S(2)}) copy-start(bf16[64,180]{1,0:T(8,128)(2,1)S(1)} %collective-permute-done.3.refs_6_) | copy-start | bytes 69124
  102.5 13.6 %all-to-all-start.4 = ((bf16[8,64,720]{2,1,0:T(8,128)(2,1)}), bf16[8,64,720]{2,1,0:T(8,128)(2,1)S(1)}, u32[]{:S(2)}, u32[]{:S(2)}) async-start(bf16[8,64,720]{2,1,0:T(8,128)(2,1)} %expert_rows.1), calls=%async_computation.4 | async-start | bytes 1572864 | tf_op jit(solution)/shard_map/all_to_all | solution.py:52
  118.0 32.3 %all-to-all-start.5 = ((bf16[32,4,720]{2,1,0:T(4,128)(2,1)}), bf16[32,4,720]{2,1,0:T(4,128)(2,1)S(1)}, u32[]{:S(2)}, u32[]{:S(2)}) async-start(bf16[32,4,720]{2,1,0:T(4,128)(2,1)} %bitcast.26), calls=%async_computation.5 | async-start | bytes 393216 | tf_op jit(solution)/shard_map/all_to_all | solution.py:52
  (3 other events, 3.3 us)

commit v3 on v2

--- a/solution.py
+++ b/solution.py
@@ -132,7 +132,7 @@
         name="expert_rows",
     )(
         expert.reshape(1).astype(jnp.int32),
-        row_block,
+        pltpu.with_memory_space_constraint(row_block, pltpu.VMEM),
         norm_gain[None],
         router.T,
         adapter_in.T,
@@ -252,11 +252,11 @@
     first = (mine[:, width].astype(jnp.int32) == expert).astype(F32)
     own_middle = lax.dynamic_slice_in_dim(mine, cut * quarter, quarter, 1).astype(F32)
     total = (total + own_middle * first[:, None]).astype(BF16)
-    total = jnp.broadcast_to(total.reshape(1, planes, CAP, quarter), (n_side, planes, CAP, quarter))
-    returned = exchange(total.reshape(n_side * planes, CAP, quarter), ("side", "z"))
-    own_hot = slot_hot(expert_routes[None], jnp.arange(n_side * planes))[:, 0]
-    out = jnp.einsum("etr,etd->rd", own_hot, returned, preferred_element_type=F32)
-    return out.astype(BF16)
+    returned = exchange(total.reshape(planes, CAP, quarter), "z")
+    own_hot = slot_hot(expert_routes[None], experts)[:, 0]
+    out = jnp.einsum("etr,etd->rd", own_hot, returned, preferred_element_type=F32).astype(BF16)
+    other = lax.ppermute(out, "side", swap)
+    return (out.astype(F32) + other.astype(F32)).astype(BF16)
 
 
 def solution(mesh):

time: 152 us -> 150 us (0.987)
  the two profiles are of different devices: /device:TPU:8 before, /device:TPU:32 now
where the time goes in v3:
time: 150 us; the launch traced here: 149 us
  starting transfers between devices  66.7 us (44%)
  waiting for transfers between devices  61.2 us (41%)
  Pallas kernels  7.87 us (5%)
  local copies, waits for them, and re-layouts  6.59 us (4%)
  other arithmetic  3.24 us (2%)
  matrix products  2.58 us (2%)
    all_to_all x6, waiting for transfers between devices, exchange(): return lax.all_to_all(array, axes, split_axis=0, concat_axis=0, tiled=True)  52.7 us
    all_to_all x6, starting transfers between devices, exchange(): return lax.all_to_all(array, axes, split_axis=0, concat_axis=0, tiled=True)  48.5 us
    ppermute x4, starting transfers between devices, shards(): lax.ppermute(part, 'core', swap)  8.18 us
    pallas_call x1, Pallas kernels, expert_rows(): pl.pallas_call(functools.partial(expert_kernel, n_ylo, n_cuts, topk), out...  7.87 us
    ppermute x3, starting transfers between devices, shards(): pieces.append(lax.ppermute(attn_proj.T, axes, flip))  7.59 us
    ppermute x1, waiting for transfers between devices, shards(): other = lax.ppermute(out, 'side', swap)  4.75 us
    ppermute x3, waiting for transfers between devices, shards(): pieces.append(lax.ppermute(attn_proj.T, axes, flip))  3.25 us
  transfers between devices with their start and end apart: 14, of which 10 were waited for; matrix products, arithmetic and copies ran while one was open for 2% of the time, Pallas kernels for 0%

profile of v3, /device:TPU:32, one launch (start us, length us, event | category | flops | bytes accessed | tf_op | source)
XLA Modules:
  0.0 148.7 jit_solution(3106829802411912635)
XLA Ops:
  5.8 15.2 %all-to-all-start = ((bf16[16,16,640]{2,1,0:T(8,128)(2,1)}), bf16[16,16,640]{2,1,0:T(8,128)(2,1)S(1)}, u32[]{:S(2)}, u32[]{:S(2)}) async-start(bf16[16,16,640]{2,1,0:T(8,128)(2,1)} %maximum_maximum_fusion), calls=%async_computation | async-start | bytes 655360 | tf_op jit(solution)/shard_map/all_to_all | solution.py:52
  21.0 1.9 %collective-permute-start = (bf16[45,512]{1,0:T(8,128)(2,1)S(1)}, bf16[45,512]{1,0:T(8,128)(2,1)S(1)}, u32[]{:S(2)}, u32[]{:S(2)}) collective-permute-start(bf16[45,512]{1,0:T(8,128)(2,1)S(1)} %bitcast.74), channel_id=1, source_target_pairs={{0,4},{4,0},{1,5},{5,1},{2,6},{6,2},{3,7},{7,3},{8,12},{12,8},{9,1... | collective-permute-start | bytes 138248 | tf_op jit(solution)/shard_map/ppermute | solution.py:183
  22.9 3.5 %collective-permute-start.1 = (bf16[45,512]{1,0:T(8,128)(2,1)S(1)}, bf16[45,512]{1,0:T(8,128)(2,1)S(1)}, u32[]{:S(2)}, u32[]{:S(2)}) collective-permute-start(bf16[45,512]{1,0:T(8,128)(2,1)S(1)} %bitcast.75), channel_id=1, source_target_pairs={{0,8},{8,0},{1,9},{9,1},{2,10},{10,2},{3,11},{11,3},{4,12},{12,4},... | collective-permute-start | bytes 138248 | tf_op jit(solution)/shard_map/ppermute | solution.py:183
  26.4 2.2 %collective-permute-start.2 = (bf16[45,512]{1,0:T(8,128)(2,1)S(1)}, bf16[45,512]{1,0:T(8,128)(2,1)S(1)}, u32[]{:S(2)}, u32[]{:S(2)}) collective-permute-start(bf16[45,512]{1,0:T(8,128)(2,1)S(1)} %bitcast.76), channel_id=1, source_target_pairs={{0,12},{4,8},{8,4},{12,0},{1,13},{5,9},{9,5},{13,1},{2,14},{6,10},... | collective-permute-start | bytes 138248 | tf_op jit(solution)/shard_map/ppermute | solution.py:183
  28.9 3.0 %collective-permute-done.2 = bf16[45,512]{1,0:T(8,128)(2,1)S(1)} collective-permute-done((bf16[45,512]{1,0:T(8,128)(2,1)S(1)}, bf16[45,512]{1,0:T(8,128)(2,1)S(1)}, u32[]{:S(2)}, u32[]{:S(2)}) %collective-permute-start.2) | collective-permute-done | bytes 46112 | tf_op jit(solution)/shard_map/ppermute | solution.py:183
  32.0 8.9 %all-to-all-done = bf16[16,16,640]{2,1,0:T(8,128)(2,1)S(1)} async-done(((bf16[16,16,640]{2,1,0:T(8,128)(2,1)}), bf16[16,16,640]{2,1,0:T(8,128)(2,1)S(1)}, u32[]{:S(2)}, u32[]{:S(2)}) %all-to-all-start) | async-done | bytes 327712 | tf_op jit(solution)/shard_map/all_to_all | solution.py:52
  42.1 6.9 %all-to-all-start.1 = ((bf16[8,64,180]{2,1,0:T(8,128)(2,1)}), bf16[8,64,180]{2,1,0:T(8,128)(2,1)S(1)}, u32[]{:S(2)}, u32[]{:S(2)}) async-start(bf16[8,64,180]{2,1,0:T(8,128)(2,1)} %bitcast.10), calls=%async_computation.1 | async-start | bytes 524288 | tf_op jit(solution)/shard_map/all_to_all | solution.py:52
  49.4 8.5 %all-to-all-done.1 = bf16[8,64,180]{2,1,0:T(8,128)(2,1)S(1)} async-done(((bf16[8,64,180]{2,1,0:T(8,128)(2,1)}), bf16[8,64,180]{2,1,0:T(8,128)(2,1)S(1)}, u32[]{:S(2)}, u32[]{:S(2)}) %all-to-all-start.1) | async-done | bytes 184352 | tf_op jit(solution)/shard_map/all_to_all | solution.py:52
  58.8 7.1 %all-to-all-start.2 = ((bf16[16,16,184]{2,1,0:T(8,128)(2,1)}), bf16[16,16,184]{2,1,0:T(8,128)(2,1)S(1)}, u32[]{:S(2)}, u32[]{:S(2)}) async-start(bf16[16,16,184]{2,1,0:T(8,128)(2,1)} %copy.58), calls=%async_computation.2 | async-start | bytes 262144 | tf_op jit(solution)/shard_map/all_to_all | solution.py:52
  65.9 1.9 %collective-permute-start.4 = (bf16[180,2880]{1,0:T(8,128)(2,1)S(1)}, bf16[180,2880]{1,0:T(8,128)(2,1)}, u32[]{:S(2)}, u32[]{:S(2)}) collective-permute-start(bf16[180,2880]{1,0:T(8,128)(2,1)S(1)} %bitcast.64), channel_id=1, source_target_pairs={{0,4},{4,0},{1,5},{5,1},{2,6},{6,2},{3,7},{7,3},{8,12},{12,8},{9,1... | collective-permute-start | bytes 3110408 | tf_op jit(solution)/shard_map/ppermute | solution.py:190
  67.8 2.4 %collective-permute-start.5 = (bf16[180,2880]{1,0:T(8,128)(2,1)}, bf16[180,2880]{1,0:T(8,128)(2,1)}, u32[]{:S(2)}, u32[]{:S(2)}) collective-permute-start(bf16[180,2880]{1,0:T(8,128)(2,1)} %bitcast.25.refs_8_), channel_id=1, source_target_pairs={{0,4},{4,0},{1,5},{5,1},{2,6},{6,2},{3,7},{7,3},{8,12},{12,8},{9,1... | collective-permute-start | bytes 3110408 | tf_op jit(solution)/shard_map/ppermute | solution.py:190
  70.2 1.9 %collective-permute-start.6 = (bf16[180,2880]{1,0:T(8,128)(2,1)}, bf16[180,2880]{1,0:T(8,128)(2,1)}, u32[]{:S(2)}, u32[]{:S(2)}) collective-permute-start(bf16[180,2880]{1,0:T(8,128)(2,1)} %refs_9_.1), channel_id=1, source_target_pairs={{0,4},{4,0},{1,5},{5,1},{2,6},{6,2},{3,7},{7,3},{8,12},{12,8},{9,1... | collective-permute-start | bytes 3110408 | tf_op jit(solution)/shard_map/ppermute | solution.py:190
  72.1 6.4 %all-to-all-done.2 = bf16[16,16,184]{2,1,0:T(8,128)(2,1)S(1)} async-done(((bf16[16,16,184]{2,1,0:T(8,128)(2,1)}), bf16[16,16,184]{2,1,0:T(8,128)(2,1)S(1)}, u32[]{:S(2)}, u32[]{:S(2)}) %all-to-all-start.2) | async-done | bytes 94240 | tf_op jit(solution)/shard_map/all_to_all | solution.py:52
  79.0 0.9 broadcast_in_dim.86
  79.9 3.5 %all-to-all-start.3 = ((bf16[8,16,2944]{2,1,0:T(8,128)(2,1)}), bf16[8,16,2944]{2,1,0:T(8,128)(2,1)S(1)}, u32[]{:S(2)}, u32[]{:S(2)}) async-start(bf16[8,16,2944]{2,1,0:T(8,128)(2,1)} %broadcast_in_dim.86), calls=%async_computation.3 | async-start | bytes 1507328 | tf_op jit(solution)/shard_map/all_to_all | solution.py:52
  83.5 1.9 %collective-permute-start.3 = (bf16[64,180]{1,0:T(8,128)(2,1)S(1)}, bf16[64,180]{1,0:T(8,128)(2,1)S(1)}, u32[]{:S(2)}, u32[]{:S(2)}) collective-permute-start(bf16[64,180]{1,0:T(8,128)(2,1)S(1)} %constant_dynamic-update-slice_fusion.refs_5_), channel_id=1, source_target_pairs={{0,4},{4,0},{1,5},{5,1},{2,6},{6,2},{3,7},{7,3},{8,12},{12,8},{9,1... | collective-permute-start | bytes 69128 | tf_op jit(solution)/shard_map/ppermute | solution.py:190
  86.6 6.7 %all-to-all-done.3 = bf16[8,16,2944]{2,1,0:T(8,128)(2,1)S(1)} async-done(((bf16[8,16,2944]{2,1,0:T(8,128)(2,1)}), bf16[8,16,2944]{2,1,0:T(8,128)(2,1)S(1)}, u32[]{:S(2)}, u32[]{:S(2)}) %all-to-all-start.3) | async-done | bytes 753696 | tf_op jit(solution)/shard_map/all_to_all | solution.py:52
  93.4 7.9 %expert_rows.1 = bf16[8,64,720]{2,1,0:T(8,128)(2,1)} custom-call(s32[1]{0:T(128)} %bitcast.refs_0_, bf16[128,2944]{1,0:T(8,128)(2,1)S(1)} %bitcast.60, f32[1,2880]{1,0:T(1,128)} %broadcast_in_dim.87.refs_2_, bf16[32,2880]{1,0:T(8,128)(2,1)} %bitcast.70, bf16[32,2880]{1,0:T(8,128)(2,1)} %bitcast.71, bf16[64,180]{1,0:T(8,128)(2,1)} %copy-done.3, ...), custom_call_target="tpu_custom_call" | custom-call | tf_op jit(solution)/shard_map/expert_rows/pallas_call | solution.py:121
  101.2 3.6 %all-to-all-start.4 = ((bf16[8,64,720]{2,1,0:T(8,128)(2,1)}), bf16[8,64,720]{2,1,0:T(8,128)(2,1)S(1)}, u32[]{:S(2)}, u32[]{:S(2)}) async-start(bf16[8,64,720]{2,1,0:T(8,128)(2,1)} %expert_rows.1), calls=%async_computation.4 | async-start | bytes 1572864 | tf_op jit(solution)/shard_map/all_to_all | solution.py:52
  105.0 9.8 %all-to-all-done.4 = bf16[8,64,720]{2,1,0:T(8,128)(2,1)S(1)} async-done(((bf16[8,64,720]{2,1,0:T(8,128)(2,1)}), bf16[8,64,720]{2,1,0:T(8,128)(2,1)S(1)}, u32[]{:S(2)}, u32[]{:S(2)}) %all-to-all-start.4) | async-done | bytes 737312 | tf_op jit(solution)/shard_map/all_to_all | solution.py:52
  115.7 12.2 %all-to-all-start.5 = ((bf16[16,4,720]{2,1,0:T(4,128)(2,1)}), bf16[16,4,720]{2,1,0:T(4,128)(2,1)S(1)}, u32[]{:S(2)}, u32[]{:S(2)}) async-start(bf16[16,4,720]{2,1,0:T(4,128)(2,1)} %reshape.168), calls=%async_computation.5 | async-start | bytes 196608 | tf_op jit(solution)/shard_map/all_to_all | solution.py:52
  128.3 12.4 %all-to-all-done.5 = bf16[16,4,720]{2,1,0:T(4,128)(2,1)S(1)} async-done(((bf16[16,4,720]{2,1,0:T(4,128)(2,1)}), bf16[16,4,720]{2,1,0:T(4,128)(2,1)S(1)}, u32[]{:S(2)}, u32[]{:S(2)}) %all-to-all-start.5) | async-done | bytes 92192 | tf_op jit(solution)/shard_map/all_to_all | solution.py:52
  140.8 2.5 %collective-permute-start.7 = (bf16[16,720]{1,0:T(8,128)(2,1)S(1)}, bf16[16,720]{1,0:T(8,128)(2,1)S(1)}, u32[]{:S(2)}, u32[]{:S(2)}) collective-permute-start(bf16[16,720]{1,0:T(8,128)(2,1)S(1)} %fusion.2), channel_id=1, source_target_pairs={{0,256},{256,0},{1,257},{257,1},{2,258},{258,2},{3,259},{259,3},{4... | collective-permute-start | bytes 69128 | tf_op jit(solution)/shard_map/ppermute | solution.py:258
  143.3 4.7 %collective-permute-done.7 = bf16[16,720]{1,0:T(8,128)(2,1)S(1)} collective-permute-done((bf16[16,720]{1,0:T(8,128)(2,1)S(1)}, bf16[16,720]{1,0:T(8,128)(2,1)S(1)}, u32[]{:S(2)}, u32[]{:S(2)}) %collective-permute-start.7) | collective-permute-done | bytes 23072 | tf_op jit(solution)/shard_map/ppermute | solution.py:258
  (87 shorter events, 12.3 us)
Async XLA Ops:
  0.0 2.9 %copy-start.11 = (f32[8]{0:T(128)S(1)}, f32[8]{0:T(128)}, u32[]{:S(2)}) copy-start(f32[8]{0:T(128)} %param.24) | copy-start | bytes 100
  0.0 3.1 %copy-start.10 = (bf16[16,64]{1,0:T(8,128)(2,1)S(1)}, bf16[16,64]{1,0:T(8,128)(2,1)}, u32[]{:S(2)}) copy-start(bf16[16,64]{1,0:T(8,128)(2,1)} %param.22) | copy-start | bytes 6148
  0.0 3.1 %copy-start.12 = (bf16[16,1,64,512]{3,2,1,0:T(8,128)(2,1)S(1)}, bf16[16,1,64,512]{3,2,1,0:T(8,128)(2,1)}, u32[]{:S(2)}) copy-start(bf16[16,1,64,512]{3,2,1,0:T(8,128)(2,1)} %param.20) | copy-start | bytes 3145732
  4.5 16.5 %copy-start.4 = (bf16[512,45]{0,1:T(8,128)(2,1)S(1)}, bf16[512,45]{0,1:T(8,128)(2,1)}, u32[]{:S(2)}) copy-start(bf16[512,45]{0,1:T(8,128)(2,1)} %param.25) | copy-start | bytes 138244
  5.8 35.1 %all-to-all-start = ((bf16[16,16,640]{2,1,0:T(8,128)(2,1)}), bf16[16,16,640]{2,1,0:T(8,128)(2,1)S(1)}, u32[]{:S(2)}, u32[]{:S(2)}) async-start(bf16[16,16,640]{2,1,0:T(8,128)(2,1)} %maximum_maximum_fusion), calls=%async_computation | async-start | bytes 655360 | tf_op jit(solution)/shard_map/all_to_all | solution.py:52
  21.0 7.7 %collective-permute-start = (bf16[45,512]{1,0:T(8,128)(2,1)S(1)}, bf16[45,512]{1,0:T(8,128)(2,1)S(1)}, u32[]{:S(2)}, u32[]{:S(2)}) collective-permute-start(bf16[45,512]{1,0:T(8,128)(2,1)S(1)} %bitcast.74), channel_id=1, source_target_pairs={{0,4},{4,0},{1,5},{5,1},{2,6},{6,2},{3,7},{7,3},{8,12},{12,8},{9,1... | collective-permute-start | bytes 138248 | tf_op jit(solution)/shard_map/ppermute | solution.py:183
  22.9 6.0 %collective-permute-start.1 = (bf16[45,512]{1,0:T(8,128)(2,1)S(1)}, bf16[45,512]{1,0:T(8,128)(2,1)S(1)}, u32[]{:S(2)}, u32[]{:S(2)}) collective-permute-start(bf16[45,512]{1,0:T(8,128)(2,1)S(1)} %bitcast.75), channel_id=1, source_target_pairs={{0,8},{8,0},{1,9},{9,1},{2,10},{10,2},{3,11},{11,3},{4,12},{12,4},... | collective-permute-start | bytes 138248 | tf_op jit(solution)/shard_map/ppermute | solution.py:183
  26.4 5.5 %collective-permute-start.2 = (bf16[45,512]{1,0:T(8,128)(2,1)S(1)}, bf16[45,512]{1,0:T(8,128)(2,1)S(1)}, u32[]{:S(2)}, u32[]{:S(2)}) collective-permute-start(bf16[45,512]{1,0:T(8,128)(2,1)S(1)} %bitcast.76), channel_id=1, source_target_pairs={{0,12},{4,8},{8,4},{12,0},{1,13},{5,9},{9,5},{13,1},{2,14},{6,10},... | collective-permute-start | bytes 138248 | tf_op jit(solution)/shard_map/ppermute | solution.py:183
  41.4 24.5 %copy-start.1 = (bf16[2880,180]{0,1:T(8,128)(2,1)S(1)}, bf16[2880,180]{0,1:T(8,128)(2,1)}, u32[]{:S(2)}) copy-start(bf16[2880,180]{0,1:T(8,128)(2,1)} %param.30) | copy-start | bytes 3110404
  42.1 15.7 %all-to-all-start.1 = ((bf16[8,64,180]{2,1,0:T(8,128)(2,1)}), bf16[8,64,180]{2,1,0:T(8,128)(2,1)S(1)}, u32[]{:S(2)}, u32[]{:S(2)}) async-start(bf16[8,64,180]{2,1,0:T(8,128)(2,1)} %bitcast.10), calls=%async_computation.1 | async-start | bytes 524288 | tf_op jit(solution)/shard_map/all_to_all | solution.py:52
  58.8 19.7 %all-to-all-start.2 = ((bf16[16,16,184]{2,1,0:T(8,128)(2,1)}), bf16[16,16,184]{2,1,0:T(8,128)(2,1)S(1)}, u32[]{:S(2)}, u32[]{:S(2)}) async-start(bf16[16,16,184]{2,1,0:T(8,128)(2,1)} %copy.58), calls=%async_computation.2 | async-start | bytes 262144 | tf_op jit(solution)/shard_map/all_to_all | solution.py:52
  65.9 20.8 %collective-permute-start.4 = (bf16[180,2880]{1,0:T(8,128)(2,1)S(1)}, bf16[180,2880]{1,0:T(8,128)(2,1)}, u32[]{:S(2)}, u32[]{:S(2)}) collective-permute-start(bf16[180,2880]{1,0:T(8,128)(2,1)S(1)} %bitcast.64), channel_id=1, source_target_pairs={{0,4},{4,0},{1,5},{5,1},{2,6},{6,2},{3,7},{7,3},{8,12},{12,8},{9,1... | collective-permute-start | bytes 3110408 | tf_op jit(solution)/shard_map/ppermute | solution.py:190
  67.8 18.8 %collective-permute-start.5 = (bf16[180,2880]{1,0:T(8,128)(2,1)}, bf16[180,2880]{1,0:T(8,128)(2,1)}, u32[]{:S(2)}, u32[]{:S(2)}) collective-permute-start(bf16[180,2880]{1,0:T(8,128)(2,1)} %bitcast.25.refs_8_), channel_id=1, source_target_pairs={{0,4},{4,0},{1,5},{5,1},{2,6},{6,2},{3,7},{7,3},{8,12},{12,8},{9,1... | collective-permute-start | bytes 3110408 | tf_op jit(solution)/shard_map/ppermute | solution.py:190
  70.2 16.4 %collective-permute-start.6 = (bf16[180,2880]{1,0:T(8,128)(2,1)}, bf16[180,2880]{1,0:T(8,128)(2,1)}, u32[]{:S(2)}, u32[]{:S(2)}) collective-permute-start(bf16[180,2880]{1,0:T(8,128)(2,1)} %refs_9_.1), channel_id=1, source_target_pairs={{0,4},{4,0},{1,5},{5,1},{2,6},{6,2},{3,7},{7,3},{8,12},{12,8},{9,1... | collective-permute-start | bytes 3110408 | tf_op jit(solution)/shard_map/ppermute | solution.py:190
  79.0 4.5 %copy-start.6 = (bf16[32,180]{1,0:T(8,128)(2,1)S(1)}, bf16[32,180]{1,0:T(8,128)(2,1)}, u32[]{:S(2)}) copy-start(bf16[32,180]{1,0:T(8,128)(2,1)} %param.34) | copy-start | bytes 34564
  79.0 4.5 %copy-start.7 = (bf16[32,180]{1,0:T(8,128)(2,1)S(1)}, bf16[32,180]{1,0:T(8,128)(2,1)}, u32[]{:S(2)}) copy-start(bf16[32,180]{1,0:T(8,128)(2,1)} %param.35) | copy-start | bytes 34564
  79.0 6.5 %copy-start.8 = (f32[2880]{0:T(1024)S(1)}, f32[2880]{0:T(1024)}, u32[]{:S(2)}) copy-start(f32[2880]{0:T(1024)} %param.27) | copy-start | bytes 34564
  79.9 13.4 %all-to-all-start.3 = ((bf16[8,16,2944]{2,1,0:T(8,128)(2,1)}), bf16[8,16,2944]{2,1,0:T(8,128)(2,1)S(1)}, u32[]{:S(2)}, u32[]{:S(2)}) async-start(bf16[8,16,2944]{2,1,0:T(8,128)(2,1)} %broadcast_in_dim.86), calls=%async_computation.3 | async-start | bytes 1507328 | tf_op jit(solution)/shard_map/all_to_all | solution.py:52
  83.5 9.8 %copy-start.3 = (bf16[64,180]{1,0:T(8,128)(2,1)}, bf16[64,180]{1,0:T(8,128)(2,1)S(1)}, u32[]{:S(2)}) copy-start(bf16[64,180]{1,0:T(8,128)(2,1)S(1)} %constant_dynamic-update-slice_fusion.refs_5_) | copy-start | bytes 69124
  83.5 3.1 %collective-permute-start.3 = (bf16[64,180]{1,0:T(8,128)(2,1)S(1)}, bf16[64,180]{1,0:T(8,128)(2,1)S(1)}, u32[]{:S(2)}, u32[]{:S(2)}) collective-permute-start(bf16[64,180]{1,0:T(8,128)(2,1)S(1)} %constant_dynamic-update-slice_fusion.refs_5_), channel_id=1, source_target_pairs={{0,4},{4,0},{1,5},{5,1},{2,6},{6,2},{3,7},{7,3},{8,12},{12,8},{9,1... | collective-permute-start | bytes 69128 | tf_op jit(solution)/shard_map/ppermute | solution.py:190
  86.6 6.7 %copy-start.5 = (bf16[64,180]{1,0:T(8,128)(2,1)}, bf16[64,180]{1,0:T(8,128)(2,1)S(1)}, u32[]{:S(2)}) copy-start(bf16[64,180]{1,0:T(8,128)(2,1)S(1)} %collective-permute-done.3.refs_6_) | copy-start | bytes 69124
  101.2 13.6 %all-to-all-start.4 = ((bf16[8,64,720]{2,1,0:T(8,128)(2,1)}), bf16[8,64,720]{2,1,0:T(8,128)(2,1)S(1)}, u32[]{:S(2)}, u32[]{:S(2)}) async-start(bf16[8,64,720]{2,1,0:T(8,128)(2,1)} %expert_rows.1), calls=%async_computation.4 | async-start | bytes 1572864 | tf_op jit(solution)/shard_map/all_to_all | solution.py:52
  115.7 24.9 %all-to-all-start.5 = ((bf16[16,4,720]{2,1,0:T(4,128)(2,1)}), bf16[16,4,720]{2,1,0:T(4,128)(2,1)S(1)}, u32[]{:S(2)}, u32[]{:S(2)}) async-start(bf16[16,4,720]{2,1,0:T(4,128)(2,1)} %reshape.168), calls=%async_computation.5 | async-start | bytes 196608 | tf_op jit(solution)/shard_map/all_to_all | solution.py:52
  140.8 7.2 %collective-permute-start.7 = (bf16[16,720]{1,0:T(8,128)(2,1)S(1)}, bf16[16,720]{1,0:T(8,128)(2,1)S(1)}, u32[]{:S(2)}, u32[]{:S(2)}) collective-permute-start(bf16[16,720]{1,0:T(8,128)(2,1)S(1)} %fusion.2), channel_id=1, source_target_pairs={{0,256},{256,0},{1,257},{257,1},{2,258},{258,2},{3,259},{259,3},{4... | collective-permute-start | bytes 69128 | tf_op jit(solution)/shard_map/ppermute | solution.py:258
  (3 other events, 5.0 us)

commit v4 on v3

--- a/solution.py
+++ b/solution.py
@@ -162,29 +162,34 @@
     adapter_gate,
     adapter_up,
 ):
-    planes = lax.axis_size("z")
+    pairs = lax.axis_size("zp")
+    planes = pairs * lax.axis_size("zq")
     n_cuts = lax.axis_size("cuts")
     n_side = lax.axis_size("side")
     n_ylo = lax.axis_size("ylo")
     side = lax.axis_index("side")
-    plane = lax.axis_index("z")
+    plane = lax.axis_index(("zp", "zq"))
+    odd = lax.axis_index("zq")
     ylo = lax.axis_index("ylo")
+    core = lax.axis_index("core")
     cut = lax.axis_index("cuts")
     rows, width = residual_in.shape
     topk = expert_routes.shape[1]
-    heads_in, piece = attn_proj.shape
-    strip = width // planes
+    heads_in, _ = attn_proj.shape
+    strip = width // pairs
+    share = strip // n_cuts
     quarter = width // n_cuts
     swap = [(0, 1), (1, 0)]
 
-    pieces = [attn_proj.T]
+    pair = [attn_proj.T, lax.ppermute(attn_proj.T, "zq", swap)]
+    pair = jnp.stack([jnp.where(odd == i, pair[0], pair[1]) for i in range(2)])
+    pieces = [pair]
     for axes in ("core", "ylo", ("ylo", "core")):
         flip = swap if isinstance(axes, str) else [(i, 3 - i) for i in range(4)]
-        pieces.append(lax.ppermute(attn_proj.T, axes, flip))
-    core = lax.axis_index("core")
+        pieces.append(lax.ppermute(pair, axes, flip))
     pieces = [jnp.where(core == 0, pieces[i], pieces[i ^ 1]) for i in range(4)]
     pieces = [jnp.where(ylo == 0, pieces[i], pieces[i ^ 2]) for i in range(4)]
-    plane_proj = jnp.concatenate(pieces, 0)
+    pair_proj = jnp.stack(pieces, 1).reshape(strip, heads_in)
     adapters = jnp.concatenate([adapter_gate, adapter_up], 0)
     hidden_own = (expert_gate.T, expert_up.T, expert_down, adapters)
     hidden_other = tuple(lax.ppermute(part, "core", swap) for part in hidden_own)
@@ -193,42 +198,43 @@
         queries, cache_keys, cache_values, new_keys, new_values, lengths, head_sinks
     )
 
-    residual = residual_in.reshape(rows, planes, n_cuts, piece)
+    residual = residual_in.reshape(rows, pairs, n_cuts, share)
     residual = lax.dynamic_index_in_dim(residual, cut, 2, keepdims=False).transpose(1, 0, 2)
     payload = jnp.concatenate(
         [
-            jnp.broadcast_to(attn_out[None], (planes, rows, heads_in)),
+            jnp.broadcast_to(attn_out[None], (pairs, rows, heads_in)),
             residual,
-            jnp.broadcast_to(expert_routes.astype(BF16)[None], (planes, rows, topk)),
-            jnp.zeros((planes, rows, 128 - piece - topk), BF16),
+            jnp.broadcast_to(expert_routes.astype(BF16)[None], (pairs, rows, topk)),
+            jnp.zeros((pairs, rows, 128 - share - topk), BF16),
         ],
         axis=2,
     )
-    held = exchange(payload, "z")
-    held = held.reshape(planes * rows, heads_in + 128)
+    held = exchange(payload, "zp")
+    held = held.reshape(pairs * rows, heads_in + 128)
     line = lax.broadcasted_iota(jnp.int32, (strip, 128), 1)
     column = lax.broadcasted_iota(jnp.int32, (strip, 128), 0)
-    residual_part = jnp.where((column == cut * piece + line) & (line < piece), 1.0 / n_side, 0.0)
-    weights = jnp.concatenate([plane_proj, residual_part.astype(BF16)], 1)
+    residual_part = jnp.where((column == cut * share + line) & (line < share), 1.0 / n_side, 0.0)
+    weights = jnp.concatenate([pair_proj, residual_part.astype(BF16)], 1)
     partial = lax.dot_general(held, weights, (((1,), (1,)), ((), ())), preferred_element_type=F32)
-    partial = partial.astype(BF16).reshape(1, n_cuts, rows * planes // n_cuts, strip)
+    partial = partial.astype(BF16).reshape(1, n_cuts, rows * pairs // n_cuts, strip)
     partial = jnp.broadcast_to(partial, (n_side,) + partial.shape[1:])
     partial = exchange(partial.reshape((n_side * n_cuts,) + partial.shape[2:]), ("side", "cuts"))
     middle = jnp.sum(partial.astype(F32), axis=0).astype(BF16)
 
-    blocks = planes // n_cuts
+    blocks = pairs // n_cuts
     experts = side * planes + jnp.arange(planes)
-    routes = held[:, heads_in + piece : heads_in + piece + topk].reshape(n_cuts, blocks, rows, topk)
+    routes = held[:, heads_in + share : heads_in + share + topk].reshape(n_cuts, blocks, rows, topk)
     routes = lax.dynamic_index_in_dim(routes, cut, 0, keepdims=False)
     hot = slot_hot(routes.astype(jnp.int32), experts)
     source = jnp.concatenate([middle.reshape(blocks, rows, strip), routes], 2)
     outgoing = jnp.einsum("zktr,krd->zktd", hot, source, preferred_element_type=F32).astype(BF16)
-    outgoing = outgoing.reshape(planes, blocks * CAP, strip + topk)
-    arrived = exchange(outgoing, "z")
-    row_part = arrived[:, :, :strip].transpose(1, 0, 2).reshape(blocks * CAP, width)
+    arrived = exchange(outgoing.reshape(planes, blocks * CAP, strip + topk), ("zp", "zq"))
+    arrived = arrived.reshape(pairs, planes // pairs, blocks, CAP, strip + topk)
+    row_part = arrived[..., :strip].transpose(2, 1, 3, 0, 4).reshape(-1, width)
+    slot_routes = arrived[0, ..., strip:].transpose(1, 0, 2, 3).reshape(-1, topk)
     lanes = -(-(width + topk) // 128) * 128
-    spare = jnp.zeros((blocks * CAP, lanes - width - topk), BF16)
-    row_part = jnp.concatenate([row_part, arrived[0, :, strip:], spare], 1)
+    spare = jnp.zeros((row_part.shape[0], lanes - width - topk), BF16)
+    row_part = jnp.concatenate([row_part, slot_routes, spare], 1)
     peers = n_ylo * n_cuts
     row_block = exchange(jnp.broadcast_to(row_part[None], (peers,) + row_part.shape), ("ylo", "cuts"))
     row_block = row_block.reshape(-1, lanes)
@@ -252,7 +258,7 @@
     first = (mine[:, width].astype(jnp.int32) == expert).astype(F32)
     own_middle = lax.dynamic_slice_in_dim(mine, cut * quarter, quarter, 1).astype(F32)
     total = (total + own_middle * first[:, None]).astype(BF16)
-    returned = exchange(total.reshape(planes, CAP, quarter), "z")
+    returned = exchange(total.reshape(planes, CAP, quarter), ("zp", "zq"))
     own_hot = slot_hot(expert_routes[None], experts)[:, 0]
     out = jnp.einsum("etr,etd->rd", own_hot, returned, preferred_element_type=F32).astype(BF16)
     other = lax.ppermute(out, "side", swap)
@@ -260,10 +266,11 @@
 
 
 def solution(mesh):
-    fine = Mesh(mesh.devices.reshape(2, 16, 2, 2, 4), ("side", "z", "ylo", "core", "cuts"))
-    group = ("z", "ylo", "core")
+    names = ("side", "zp", "zq", "ylo", "core", "cuts")
+    fine = Mesh(mesh.devices.reshape(2, 8, 2, 2, 2, 4), names)
+    group = ("zp", "zq", "ylo", "core")
     heads = ("side", "cuts")
-    hidden = ("side", "z", "ylo", "core", "cuts")
+    hidden = names
     placed = (
         P(group, heads),
         P(group, heads, None, None),

time: 150 us -> 149 us (level)
  waiting for transfers between devices: 61.2 us -> 58.5 us
  starting transfers between devices: 66.7 us -> 68.9 us
    ppermute x3 -> x4, starting transfers between devices: 7.59 us -> 15.1 us  [the longest x3 7.59 us: shards(): pieces.append(lax.ppermute(pair, axes, flip))]
    all_to_all x6, starting transfers between devices: 48.5 us -> 43.2 us  [exchange(): return lax.all_to_all(array, axes, split_axis=0, concat_axis=0, tiled=True)]
    all_to_all x6, waiting for transfers between devices: 52.7 us -> 48.8 us  [exchange(): return lax.all_to_all(array, axes, split_axis=0, concat_axis=0, tiled=True)]
    ppermute x3 -> x4, waiting for transfers between devices: 3.25 us -> 4.38 us  [the longest x3 4.38 us: shards(): pieces.append(lax.ppermute(pair, axes, flip))]
  transfers between devices with their start and end apart: 14 -> 15, of which waited for: 10 -> 10; matrix products, arithmetic and copies ran while one was open for 2% -> 6% of each run, Pallas kernels for 0% -> 0%
where the time goes in v4:
time: 149 us; the launch traced here: 148 us
  starting transfers between devices  68.9 us (46%)
  waiting for transfers between devices  58.5 us (39%)
  Pallas kernels  7.86 us (5%)
  local copies, waits for them, and re-layouts  6.47 us (4%)
  other arithmetic  3.13 us (2%)
  matrix products  2.58 us (2%)
    all_to_all x6, waiting for transfers between devices, exchange(): return lax.all_to_all(array, axes, split_axis=0, concat_axis=0, tiled=True)  48.8 us
    all_to_all x6, starting transfers between devices, exchange(): return lax.all_to_all(array, axes, split_axis=0, concat_axis=0, tiled=True)  43.2 us
    ppermute x4, starting transfers between devices, shards(): lax.ppermute(part, 'core', swap)  8.18 us
    pallas_call x1, Pallas kernels, expert_rows(): pl.pallas_call(functools.partial(expert_kernel, n_ylo, n_cuts, topk), out...  7.86 us
    ppermute x3, starting transfers between devices, shards(): pieces.append(lax.ppermute(pair, axes, flip))  7.59 us
    ppermute x1, starting transfers between devices, shards(): pair = [attn_proj.T, lax.ppermute(attn_proj.T, 'zq', swap)]  7.49 us
    ppermute x1, waiting for transfers between devices, shards(): other = lax.ppermute(out, 'side', swap)  4.75 us
    ppermute x3, waiting for transfers between devices, shards(): pieces.append(lax.ppermute(pair, axes, flip))  4.38 us
  transfers between devices with their start and end apart: 15, of which 10 were waited for; matrix products, arithmetic and copies ran while one was open for 6% of the time, Pallas kernels for 0%

profile of v4, /device:TPU:32, one launch (start us, length us, event | category | flops | bytes accessed | tf_op | source)
XLA Modules:
  0.0 148.0 jit_solution(1106394613186397096)
XLA Ops:
  0.0 7.5 %collective-permute-start = (bf16[45,512]{1,0:T(8,128)(2,1)}, bf16[45,512]{1,0:T(8,128)(2,1)S(1)}, u32[]{:S(2)}, u32[]{:S(2)}) collective-permute-start(bf16[45,512]{1,0:T(8,128)(2,1)} %bitcast.88), channel_id=1, source_target_pairs={{0,16},{16,0},{1,17},{17,1},{2,18},{18,2},{3,19},{19,3},{4,20},{20... | collective-permute-start | bytes 138248 | tf_op jit(solution)/shard_map/ppermute | solution.py:184
  12.7 9.8 %all-to-all-start = ((bf16[8,16,640]{2,1,0:T(8,128)(2,1)}), bf16[8,16,640]{2,1,0:T(8,128)(2,1)S(1)}, u32[]{:S(2)}, u32[]{:S(2)}) async-start(bf16[8,16,640]{2,1,0:T(8,128)(2,1)} %maximum_maximum_fusion), calls=%async_computation | async-start | bytes 327680 | tf_op jit(solution)/shard_map/all_to_all | solution.py:52
  22.6 1.9 %collective-permute-start.1 = (bf16[2,45,512]{2,1,0:T(8,128)(2,1)S(1)}, bf16[2,45,512]{2,1,0:T(8,128)(2,1)S(1)}, u32[]{:S(2)}, u32[]{:S(2)}) collective-permute-start(bf16[2,45,512]{2,1,0:T(8,128)(2,1)S(1)} %pad_maximum_fusion.1), channel_id=1, source_target_pairs={{0,4},{4,0},{1,5},{5,1},{2,6},{6,2},{3,7},{7,3},{8,12},{12,8},{9,1... | collective-permute-start | bytes 276488 | tf_op jit(solution)/shard_map/ppermute | solution.py:189
  24.5 3.5 %collective-permute-start.2 = (bf16[2,45,512]{2,1,0:T(8,128)(2,1)S(1)}, bf16[2,45,512]{2,1,0:T(8,128)(2,1)S(1)}, u32[]{:S(2)}, u32[]{:S(2)}) collective-permute-start(bf16[2,45,512]{2,1,0:T(8,128)(2,1)S(1)} %pad_maximum_fusion.1), channel_id=1, source_target_pairs={{0,8},{8,0},{1,9},{9,1},{2,10},{10,2},{3,11},{11,3},{4,12},{12,4},... | collective-permute-start | bytes 276488 | tf_op jit(solution)/shard_map/ppermute | solution.py:189
  28.0 2.2 %collective-permute-start.3 = (bf16[2,45,512]{2,1,0:T(8,128)(2,1)S(1)}, bf16[2,45,512]{2,1,0:T(8,128)(2,1)S(1)}, u32[]{:S(2)}, u32[]{:S(2)}) collective-permute-start(bf16[2,45,512]{2,1,0:T(8,128)(2,1)S(1)} %pad_maximum_fusion.1), channel_id=1, source_target_pairs={{0,12},{4,8},{8,4},{12,0},{1,13},{5,9},{9,5},{13,1},{2,14},{6,10},... | collective-permute-start | bytes 276488 | tf_op jit(solution)/shard_map/ppermute | solution.py:189
  31.6 3.0 %collective-permute-done.3 = bf16[2,45,512]{2,1,0:T(8,128)(2,1)S(1)} collective-permute-done((bf16[2,45,512]{2,1,0:T(8,128)(2,1)S(1)}, bf16[2,45,512]{2,1,0:T(8,128)(2,1)S(1)}, u32[]{:S(2)}, u32[]{:S(2)}) %collective-permute-start.3) | collective-permute-done | bytes 92192 | tf_op jit(solution)/shard_map/ppermute | solution.py:189
  34.9 3.8 %all-to-all-done = bf16[8,16,640]{2,1,0:T(8,128)(2,1)S(1)} async-done(((bf16[8,16,640]{2,1,0:T(8,128)(2,1)}), bf16[8,16,640]{2,1,0:T(8,128)(2,1)S(1)}, u32[]{:S(2)}, u32[]{:S(2)}) %all-to-all-start) | async-done | bytes 163872 | tf_op jit(solution)/shard_map/all_to_all | solution.py:52
  40.0 6.9 %all-to-all-start.1 = ((bf16[8,32,360]{2,1,0:T(8,128)(2,1)}), bf16[8,32,360]{2,1,0:T(8,128)(2,1)S(1)}, u32[]{:S(2)}, u32[]{:S(2)}) async-start(bf16[8,32,360]{2,1,0:T(8,128)(2,1)} %bitcast.16), calls=%async_computation.1 | async-start | bytes 393216 | tf_op jit(solution)/shard_map/all_to_all | solution.py:52
  47.3 8.0 %all-to-all-done.1 = bf16[8,32,360]{2,1,0:T(8,128)(2,1)S(1)} async-done(((bf16[8,32,360]{2,1,0:T(8,128)(2,1)}), bf16[8,32,360]{2,1,0:T(8,128)(2,1)S(1)}, u32[]{:S(2)}, u32[]{:S(2)}) %all-to-all-start.1) | async-done | bytes 184352 | tf_op jit(solution)/shard_map/all_to_all | solution.py:52
  56.3 8.9 %all-to-all-start.2 = ((bf16[16,8,364]{2,1,0:T(8,128)(2,1)}), bf16[16,8,364]{2,1,0:T(8,128)(2,1)S(1)}, u32[]{:S(2)}, u32[]{:S(2)}) async-start(bf16[16,8,364]{2,1,0:T(8,128)(2,1)} %copy.80), calls=%async_computation.2 | async-start | bytes 196608 | tf_op jit(solution)/shard_map/all_to_all | solution.py:52
  65.2 1.9 %collective-permute-start.5 = (bf16[180,2880]{1,0:T(8,128)(2,1)S(1)}, bf16[180,2880]{1,0:T(8,128)(2,1)}, u32[]{:S(2)}, u32[]{:S(2)}) collective-permute-start(bf16[180,2880]{1,0:T(8,128)(2,1)S(1)} %bitcast.78), channel_id=1, source_target_pairs={{0,4},{4,0},{1,5},{5,1},{2,6},{6,2},{3,7},{7,3},{8,12},{12,8},{9,1... | collective-permute-start | bytes 3110408 | tf_op jit(solution)/shard_map/ppermute | solution.py:195
  67.1 2.4 %collective-permute-start.6 = (bf16[180,2880]{1,0:T(8,128)(2,1)}, bf16[180,2880]{1,0:T(8,128)(2,1)}, u32[]{:S(2)}, u32[]{:S(2)}) collective-permute-start(bf16[180,2880]{1,0:T(8,128)(2,1)} %bitcast.33.refs_8_), channel_id=1, source_target_pairs={{0,4},{4,0},{1,5},{5,1},{2,6},{6,2},{3,7},{7,3},{8,12},{12,8},{9,1... | collective-permute-start | bytes 3110408 | tf_op jit(solution)/shard_map/ppermute | solution.py:195
  69.5 1.9 %collective-permute-start.7 = (bf16[180,2880]{1,0:T(8,128)(2,1)}, bf16[180,2880]{1,0:T(8,128)(2,1)}, u32[]{:S(2)}, u32[]{:S(2)}) collective-permute-start(bf16[180,2880]{1,0:T(8,128)(2,1)} %refs_9_.1), channel_id=1, source_target_pairs={{0,4},{4,0},{1,5},{5,1},{2,6},{6,2},{3,7},{7,3},{8,12},{12,8},{9,1... | collective-permute-start | bytes 3110408 | tf_op jit(solution)/shard_map/ppermute | solution.py:195
  71.5 5.9 %all-to-all-done.2 = bf16[16,8,364]{2,1,0:T(8,128)(2,1)S(1)} async-done(((bf16[16,8,364]{2,1,0:T(8,128)(2,1)}), bf16[16,8,364]{2,1,0:T(8,128)(2,1)S(1)}, u32[]{:S(2)}, u32[]{:S(2)}) %all-to-all-start.2) | async-done | bytes 93216 | tf_op jit(solution)/shard_map/all_to_all | solution.py:52
  78.7 3.5 %all-to-all-start.3 = ((bf16[8,16,2944]{2,1,0:T(8,128)(2,1)}), bf16[8,16,2944]{2,1,0:T(8,128)(2,1)S(1)}, u32[]{:S(2)}, u32[]{:S(2)}) async-start(bf16[8,16,2944]{2,1,0:T(8,128)(2,1)} %broadcast_in_dim.86), calls=%async_computation.3 | async-start | bytes 1507328 | tf_op jit(solution)/shard_map/all_to_all | solution.py:52
  82.3 1.9 %collective-permute-start.4 = (bf16[64,180]{1,0:T(8,128)(2,1)S(1)}, bf16[64,180]{1,0:T(8,128)(2,1)S(1)}, u32[]{:S(2)}, u32[]{:S(2)}) collective-permute-start(bf16[64,180]{1,0:T(8,128)(2,1)S(1)} %constant_dynamic-update-slice_fusion.refs_5_), channel_id=1, source_target_pairs={{0,4},{4,0},{1,5},{5,1},{2,6},{6,2},{3,7},{7,3},{8,12},{12,8},{9,1... | collective-permute-start | bytes 69128 | tf_op jit(solution)/shard_map/ppermute | solution.py:195
  85.4 7.2 %all-to-all-done.3 = bf16[8,16,2944]{2,1,0:T(8,128)(2,1)S(1)} async-done(((bf16[8,16,2944]{2,1,0:T(8,128)(2,1)}), bf16[8,16,2944]{2,1,0:T(8,128)(2,1)S(1)}, u32[]{:S(2)}, u32[]{:S(2)}) %all-to-all-start.3) | async-done | bytes 753696 | tf_op jit(solution)/shard_map/all_to_all | solution.py:52
  92.6 7.9 %expert_rows.1 = bf16[8,64,720]{2,1,0:T(8,128)(2,1)} custom-call(s32[1]{0:T(128)} %bitcast.refs_0_, bf16[128,2944]{1,0:T(8,128)(2,1)S(1)} %bitcast.74, f32[1,2880]{1,0:T(1,128)} %broadcast_in_dim.87.refs_2_, bf16[32,2880]{1,0:T(8,128)(2,1)} %bitcast.83, bf16[32,2880]{1,0:T(8,128)(2,1)} %bitcast.84, bf16[64,180]{1,0:T(8,128)(2,1)} %copy-done.3, ...), custom_call_target="tpu_custom_call" | custom-call | tf_op jit(solution)/shard_map/expert_rows/pallas_call | solution.py:121
  100.5 3.6 %all-to-all-start.4 = ((bf16[8,64,720]{2,1,0:T(8,128)(2,1)}), bf16[8,64,720]{2,1,0:T(8,128)(2,1)S(1)}, u32[]{:S(2)}, u32[]{:S(2)}) async-start(bf16[8,64,720]{2,1,0:T(8,128)(2,1)} %expert_rows.1), calls=%async_computation.4 | async-start | bytes 1572864 | tf_op jit(solution)/shard_map/all_to_all | solution.py:52
  104.3 11.6 %all-to-all-done.4 = bf16[8,64,720]{2,1,0:T(8,128)(2,1)S(1)} async-done(((bf16[8,64,720]{2,1,0:T(8,128)(2,1)}), bf16[8,64,720]{2,1,0:T(8,128)(2,1)S(1)}, u32[]{:S(2)}, u32[]{:S(2)}) %all-to-all-start.4) | async-done | bytes 737312 | tf_op jit(solution)/shard_map/all_to_all | solution.py:52
  116.7 10.4 %all-to-all-start.5 = ((bf16[16,4,720]{2,1,0:T(4,128)(2,1)}), bf16[16,4,720]{2,1,0:T(4,128)(2,1)S(1)}, u32[]{:S(2)}, u32[]{:S(2)}) async-start(bf16[16,4,720]{2,1,0:T(4,128)(2,1)} %reshape.180), calls=%async_computation.5 | async-start | bytes 196608 | tf_op jit(solution)/shard_map/all_to_all | solution.py:52
  127.6 12.4 %all-to-all-done.5 = bf16[16,4,720]{2,1,0:T(4,128)(2,1)S(1)} async-done(((bf16[16,4,720]{2,1,0:T(4,128)(2,1)}), bf16[16,4,720]{2,1,0:T(4,128)(2,1)S(1)}, u32[]{:S(2)}, u32[]{:S(2)}) %all-to-all-start.5) | async-done | bytes 92192 | tf_op jit(solution)/shard_map/all_to_all | solution.py:52
  140.1 2.5 %collective-permute-start.8 = (bf16[16,720]{1,0:T(8,128)(2,1)S(1)}, bf16[16,720]{1,0:T(8,128)(2,1)S(1)}, u32[]{:S(2)}, u32[]{:S(2)}) collective-permute-start(bf16[16,720]{1,0:T(8,128)(2,1)S(1)} %fusion.2), channel_id=1, source_target_pairs={{0,256},{256,0},{1,257},{257,1},{2,258},{258,2},{3,259},{259,3},{4... | collective-permute-start | bytes 69128 | tf_op jit(solution)/shard_map/ppermute | solution.py:264
  142.6 4.7 %collective-permute-done.8 = bf16[16,720]{1,0:T(8,128)(2,1)S(1)} collective-permute-done((bf16[16,720]{1,0:T(8,128)(2,1)S(1)}, bf16[16,720]{1,0:T(8,128)(2,1)S(1)}, u32[]{:S(2)}, u32[]{:S(2)}) %collective-permute-start.8) | collective-permute-done | bytes 23072 | tf_op jit(solution)/shard_map/ppermute | solution.py:264
  (98 shorter events, 14.1 us)
Async XLA Ops:
  0.0 9.9 %copy-start = (bf16[16,1,64,512]{3,2,1,0:T(8,128)(2,1)S(1)}, bf16[16,1,64,512]{3,2,1,0:T(8,128)(2,1)}, u32[]{:S(2)}) copy-start(bf16[16,1,64,512]{3,2,1,0:T(8,128)(2,1)} %param.19) | copy-start | bytes 3145732
  0.0 10.2 %copy-start.11 = (f32[8]{0:T(128)S(1)}, f32[8]{0:T(128)}, u32[]{:S(2)}) copy-start(f32[8]{0:T(128)} %param.24) | copy-start | bytes 100
  0.0 10.5 %copy-start.10 = (bf16[16,64]{1,0:T(8,128)(2,1)S(1)}, bf16[16,64]{1,0:T(8,128)(2,1)}, u32[]{:S(2)}) copy-start(bf16[16,64]{1,0:T(8,128)(2,1)} %param.22) | copy-start | bytes 6148
  0.0 10.5 %copy-start.12 = (bf16[16,1,64,512]{3,2,1,0:T(8,128)(2,1)S(1)}, bf16[16,1,64,512]{3,2,1,0:T(8,128)(2,1)}, u32[]{:S(2)}) copy-start(bf16[16,1,64,512]{3,2,1,0:T(8,128)(2,1)} %param.20) | copy-start | bytes 3145732
  0.0 22.5 %collective-permute-start = (bf16[45,512]{1,0:T(8,128)(2,1)}, bf16[45,512]{1,0:T(8,128)(2,1)S(1)}, u32[]{:S(2)}, u32[]{:S(2)}) collective-permute-start(bf16[45,512]{1,0:T(8,128)(2,1)} %bitcast.88), channel_id=1, source_target_pairs={{0,16},{16,0},{1,17},{17,1},{2,18},{18,2},{3,19},{19,3},{4,20},{20... | collective-permute-start | bytes 138248 | tf_op jit(solution)/shard_map/ppermute | solution.py:184
  11.0 11.6 %copy-start.4 = (bf16[512,45]{0,1:T(8,128)(2,1)S(1)}, bf16[512,45]{0,1:T(8,128)(2,1)}, u32[]{:S(2)}) copy-start(bf16[512,45]{0,1:T(8,128)(2,1)} %param.25) | copy-start | bytes 138244
  12.7 26.0 %all-to-all-start = ((bf16[8,16,640]{2,1,0:T(8,128)(2,1)}), bf16[8,16,640]{2,1,0:T(8,128)(2,1)S(1)}, u32[]{:S(2)}, u32[]{:S(2)}) async-start(bf16[8,16,640]{2,1,0:T(8,128)(2,1)} %maximum_maximum_fusion), calls=%async_computation | async-start | bytes 327680 | tf_op jit(solution)/shard_map/all_to_all | solution.py:52
  22.6 7.6 %collective-permute-start.1 = (bf16[2,45,512]{2,1,0:T(8,128)(2,1)S(1)}, bf16[2,45,512]{2,1,0:T(8,128)(2,1)S(1)}, u32[]{:S(2)}, u32[]{:S(2)}) collective-permute-start(bf16[2,45,512]{2,1,0:T(8,128)(2,1)S(1)} %pad_maximum_fusion.1), channel_id=1, source_target_pairs={{0,4},{4,0},{1,5},{5,1},{2,6},{6,2},{3,7},{7,3},{8,12},{12,8},{9,1... | collective-permute-start | bytes 276488 | tf_op jit(solution)/shard_map/ppermute | solution.py:189
  24.5 7.1 %collective-permute-start.2 = (bf16[2,45,512]{2,1,0:T(8,128)(2,1)S(1)}, bf16[2,45,512]{2,1,0:T(8,128)(2,1)S(1)}, u32[]{:S(2)}, u32[]{:S(2)}) collective-permute-start(bf16[2,45,512]{2,1,0:T(8,128)(2,1)S(1)} %pad_maximum_fusion.1), channel_id=1, source_target_pairs={{0,8},{8,0},{1,9},{9,1},{2,10},{10,2},{3,11},{11,3},{4,12},{12,4},... | collective-permute-start | bytes 276488 | tf_op jit(solution)/shard_map/ppermute | solution.py:189
  28.0 6.6 %collective-permute-start.3 = (bf16[2,45,512]{2,1,0:T(8,128)(2,1)S(1)}, bf16[2,45,512]{2,1,0:T(8,128)(2,1)S(1)}, u32[]{:S(2)}, u32[]{:S(2)}) collective-permute-start(bf16[2,45,512]{2,1,0:T(8,128)(2,1)S(1)} %pad_maximum_fusion.1), channel_id=1, source_target_pairs={{0,12},{4,8},{8,4},{12,0},{1,13},{5,9},{9,5},{13,1},{2,14},{6,10},... | collective-permute-start | bytes 276488 | tf_op jit(solution)/shard_map/ppermute | solution.py:189
  39.1 26.1 %copy-start.1 = (bf16[2880,180]{0,1:T(8,128)(2,1)S(1)}, bf16[2880,180]{0,1:T(8,128)(2,1)}, u32[]{:S(2)}) copy-start(bf16[2880,180]{0,1:T(8,128)(2,1)} %param.30) | copy-start | bytes 3110404
  40.0 15.4 %all-to-all-start.1 = ((bf16[8,32,360]{2,1,0:T(8,128)(2,1)}), bf16[8,32,360]{2,1,0:T(8,128)(2,1)S(1)}, u32[]{:S(2)}, u32[]{:S(2)}) async-start(bf16[8,32,360]{2,1,0:T(8,128)(2,1)} %bitcast.16), calls=%async_computation.1 | async-start | bytes 393216 | tf_op jit(solution)/shard_map/all_to_all | solution.py:52
  56.3 21.1 %all-to-all-start.2 = ((bf16[16,8,364]{2,1,0:T(8,128)(2,1)}), bf16[16,8,364]{2,1,0:T(8,128)(2,1)S(1)}, u32[]{:S(2)}, u32[]{:S(2)}) async-start(bf16[16,8,364]{2,1,0:T(8,128)(2,1)} %copy.80), calls=%async_computation.2 | async-start | bytes 196608 | tf_op jit(solution)/shard_map/all_to_all | solution.py:52
  65.2 20.2 %collective-permute-start.5 = (bf16[180,2880]{1,0:T(8,128)(2,1)S(1)}, bf16[180,2880]{1,0:T(8,128)(2,1)}, u32[]{:S(2)}, u32[]{:S(2)}) collective-permute-start(bf16[180,2880]{1,0:T(8,128)(2,1)S(1)} %bitcast.78), channel_id=1, source_target_pairs={{0,4},{4,0},{1,5},{5,1},{2,6},{6,2},{3,7},{7,3},{8,12},{12,8},{9,1... | collective-permute-start | bytes 3110408 | tf_op jit(solution)/shard_map/ppermute | solution.py:195
  67.1 18.3 %collective-permute-start.6 = (bf16[180,2880]{1,0:T(8,128)(2,1)}, bf16[180,2880]{1,0:T(8,128)(2,1)}, u32[]{:S(2)}, u32[]{:S(2)}) collective-permute-start(bf16[180,2880]{1,0:T(8,128)(2,1)} %bitcast.33.refs_8_), channel_id=1, source_target_pairs={{0,4},{4,0},{1,5},{5,1},{2,6},{6,2},{3,7},{7,3},{8,12},{12,8},{9,1... | collective-permute-start | bytes 3110408 | tf_op jit(solution)/shard_map/ppermute | solution.py:195
  69.5 15.9 %collective-permute-start.7 = (bf16[180,2880]{1,0:T(8,128)(2,1)}, bf16[180,2880]{1,0:T(8,128)(2,1)}, u32[]{:S(2)}, u32[]{:S(2)}) collective-permute-start(bf16[180,2880]{1,0:T(8,128)(2,1)} %refs_9_.1), channel_id=1, source_target_pairs={{0,4},{4,0},{1,5},{5,1},{2,6},{6,2},{3,7},{7,3},{8,12},{12,8},{9,1... | collective-permute-start | bytes 3110408 | tf_op jit(solution)/shard_map/ppermute | solution.py:195
  77.8 6.5 %copy-start.8 = (f32[2880]{0:T(1024)S(1)}, f32[2880]{0:T(1024)}, u32[]{:S(2)}) copy-start(f32[2880]{0:T(1024)} %param.27) | copy-start | bytes 34564
  78.7 13.9 %all-to-all-start.3 = ((bf16[8,16,2944]{2,1,0:T(8,128)(2,1)}), bf16[8,16,2944]{2,1,0:T(8,128)(2,1)S(1)}, u32[]{:S(2)}, u32[]{:S(2)}) async-start(bf16[8,16,2944]{2,1,0:T(8,128)(2,1)} %broadcast_in_dim.86), calls=%async_computation.3 | async-start | bytes 1507328 | tf_op jit(solution)/shard_map/all_to_all | solution.py:52
  82.3 10.4 %copy-start.3 = (bf16[64,180]{1,0:T(8,128)(2,1)}, bf16[64,180]{1,0:T(8,128)(2,1)S(1)}, u32[]{:S(2)}) copy-start(bf16[64,180]{1,0:T(8,128)(2,1)S(1)} %constant_dynamic-update-slice_fusion.refs_5_) | copy-start | bytes 69124
  82.3 3.1 %collective-permute-start.4 = (bf16[64,180]{1,0:T(8,128)(2,1)S(1)}, bf16[64,180]{1,0:T(8,128)(2,1)S(1)}, u32[]{:S(2)}, u32[]{:S(2)}) collective-permute-start(bf16[64,180]{1,0:T(8,128)(2,1)S(1)} %constant_dynamic-update-slice_fusion.refs_5_), channel_id=1, source_target_pairs={{0,4},{4,0},{1,5},{5,1},{2,6},{6,2},{3,7},{7,3},{8,12},{12,8},{9,1... | collective-permute-start | bytes 69128 | tf_op jit(solution)/shard_map/ppermute | solution.py:195
  85.4 7.2 %copy-start.5 = (bf16[64,180]{1,0:T(8,128)(2,1)}, bf16[64,180]{1,0:T(8,128)(2,1)S(1)}, u32[]{:S(2)}) copy-start(bf16[64,180]{1,0:T(8,128)(2,1)S(1)} %collective-permute-done.4.refs_6_) | copy-start | bytes 69124
  100.5 15.3 %all-to-all-start.4 = ((bf16[8,64,720]{2,1,0:T(8,128)(2,1)}), bf16[8,64,720]{2,1,0:T(8,128)(2,1)S(1)}, u32[]{:S(2)}, u32[]{:S(2)}) async-start(bf16[8,64,720]{2,1,0:T(8,128)(2,1)} %expert_rows.1), calls=%async_computation.4 | async-start | bytes 1572864 | tf_op jit(solution)/shard_map/all_to_all | solution.py:52
  116.7 23.2 %all-to-all-start.5 = ((bf16[16,4,720]{2,1,0:T(4,128)(2,1)}), bf16[16,4,720]{2,1,0:T(4,128)(2,1)S(1)}, u32[]{:S(2)}, u32[]{:S(2)}) async-start(bf16[16,4,720]{2,1,0:T(4,128)(2,1)} %reshape.180), calls=%async_computation.5 | async-start | bytes 196608 | tf_op jit(solution)/shard_map/all_to_all | solution.py:52
  140.1 7.2 %collective-permute-start.8 = (bf16[16,720]{1,0:T(8,128)(2,1)S(1)}, bf16[16,720]{1,0:T(8,128)(2,1)S(1)}, u32[]{:S(2)}, u32[]{:S(2)}) collective-permute-start(bf16[16,720]{1,0:T(8,128)(2,1)S(1)} %fusion.2), channel_id=1, source_target_pairs={{0,256},{256,0},{1,257},{257,1},{2,258},{258,2},{3,259},{259,3},{4... | collective-permute-start | bytes 69128 | tf_op jit(solution)/shard_map/ppermute | solution.py:264
  (4 other events, 11.1 us)
